TPU v7x, 32 devices: a whole 2x2x4 slice. The times are simulated.
32 devices in a mesh: src: 4 (over y, x), tgt: 8 (over z, core).
Axes of the slice: x: 2, y: 2, z: 4, core: 2. Of those that a mesh axis runs over, the one named last changes fastest.
Arguments:
- src_codes: bfloat16 [1024, 6144], P('tgt', 'src'), may hold values from -1 to 1
- src_scale: float32 [6144], P('src'), may hold values from 0.8 to 1.25
- tgt_codes: bfloat16 [1024, 8192], P('src', 'tgt'), may hold values from -1 to 1
- tgt_scale: float32 [8192], P('tgt'), may hold values from 0.8 to 1.25
Outputs:
- forward_best: float32 [4, 6144], P(None, 'src')
- backward_best: float32 [4, 8192], P(None, 'tgt')
All inputs are finite; a program needn't handle non-finite values.
Results may differ from a plain program's by a relative error of at most 0.0003.
Values may be sent and summed in bfloat16 or wider, within the bound.
No kernel may reach another device: no remote copies, remote signals or barrier semaphores. Data moves between devices by JAX's collectives and lax.ppermute only.
A program may use at most 64 MiB of HBM per device.

v0:
```python
import functools
import math

import jax
import jax.numpy as jnp
from jax import lax
from jax.experimental import pallas as pl
from jax.experimental.pallas import tpu as pltpu
from jax.sharding import PartitionSpec as P


TOP = 4
LANES = 128
GROUP = 512
ANY = pl.BlockSpec(memory_space=pl.ANY)
VMEM = pl.BlockSpec(memory_space=pltpu.VMEM)


def params(mib):
    return pltpu.CompilerParams(vmem_limit_bytes=mib << 20)


def exchange(a, b):
    return jnp.maximum(a, b), jnp.minimum(a, b)


def sort4(v):
    a, b, c, d = v
    a, b = exchange(a, b)
    c, d = exchange(c, d)
    a, c = exchange(a, c)
    b, d = exchange(b, d)
    b, c = exchange(b, c)
    return [a, b, c, d]


def merge4(p, q):
    m = [jnp.maximum(p[k], q[TOP - 1 - k]) for k in range(TOP)]
    m[0], m[2] = exchange(m[0], m[2])
    m[1], m[3] = exchange(m[1], m[3])
    m[0], m[1] = exchange(m[0], m[1])
    m[2], m[3] = exchange(m[2], m[3])
    return m


def over_sublanes(lists):
    for shift in (4, 2, 1):
        lists = merge4(lists, [pltpu.roll(x, shift, 0) for x in lists])
    return lists


def sweep_block(load, base, rows, first, lists, state):
    for r in range(0, rows, 32):
        v = [[load(r + 8 * a, b) for b in range(4)] for a in range(4)]
        for b in range(4):
            lists[b] = merge4(lists[b], sort4([v[a][b] for a in range(4)]))
        for a in range(4):
            s = sort4(v[a])
            at = pl.ds(base + (r + 8 * a), 8)
            if not first:
                s = merge4(s, [state[k, at, :] for k in range(TOP)])
            for k in range(TOP):
                state[k, at, :] = s[k]
    return lists


def loop_lists(count, body, write, group):
    def step(q, carried):
        lists = body(q, [list(carried[4 * b : 4 * b + 4]) for b in range(4)])
        return tuple(x for one in lists for x in one)

    empty = tuple(jnp.full((8, LANES), -jnp.inf, jnp.float32) for _ in range(16))
    lists = lax.fori_loop(0, count, step, empty)
    for b in range(4):
        best = over_sublanes(list(lists[4 * b : 4 * b + 4]))
        for k in range(TOP):
            write(k, group * 4 + b, best[k][0:1, :])


def finish_rows(rows, write, state):
    chunks = rows // LANES
    unroll = math.gcd(chunks, 8)

    def one(c):
        x = [state[k, pl.ds(c * LANES, LANES), :].T for k in range(TOP)]
        lists = [[x[k][8 * g : 8 * g + 8, :] for k in range(TOP)] for g in range(LANES // 8)]
        while len(lists) > 1:
            lists = [merge4(lists[i], lists[i + 1]) for i in range(0, len(lists), 2)]
        best = over_sublanes(lists[0])
        for k in range(TOP):
            write(k, c, best[k][0:1, :])

    def body(q, _):
        for h in range(unroll):
            one(q * unroll + h)
        return 0

    lax.fori_loop(0, chunks // unroll, body, 0)


def column_of(row):
    return jnp.broadcast_to(row, (LANES, LANES)).T


def piece_copies(z, core, depth, buf, sem, own, steps):
    copies = []

    def copy(piece, block, place):
        rows = piece.shape[0]
        at = pl.multiple_of((block * 2 + place) * rows, rows)
        return pltpu.make_async_copy(piece, buf.at[pl.ds(at, rows), :], sem.at[len(copies)])

    for place, piece in zip((core, 1 - core), own):
        copies.append((None, copy(piece, z, place)))
    for k, four in steps.items():
        for j in range(2):
            upward = core == j
            block = jnp.where(upward, z - k, z + k)
            valid = jnp.logical_and(block >= 0, block < depth)
            for h in range(2):
                copies.append((valid, copy(four[2 * j + h], block, jnp.where(upward, h, 1 - h))))

    def each(act):
        for valid, c in copies:
            if valid is None:
                act(c)
            else:
                pl.when(valid)(functools.partial(act, c))

    return each


def prep_kernel(masks, depth, steps, first, counts, *refs):
    n, m = counts
    tgt, src = refs[:n], refs[n : n + m]
    if first:
        scale_s, scale_t, tgt_buf, src_buf, column, lane, here_s, here_t, tgt_sem, src_sem, scale_sem = refs[n + m :]
    else:
        _, _, tgt_buf, src_buf, tgt_sem, src_sem = refs[n + m :]
    t, s = lax.axis_index("tgt"), lax.axis_index("src")
    core, z = t % 2, t // 2
    height = tgt[0].shape[0]
    copies = []
    for i in range(n):
        at = jnp.where(core == 0, s ^ masks[i][0], s ^ masks[i][1]) * height
        copies.append(pltpu.make_async_copy(
            tgt[i], tgt_buf.at[pl.ds(pl.multiple_of(at, height), height), :], tgt_sem.at[i]))
    own = 2 if first else 0
    each = piece_copies(z, core, depth, src_buf, src_sem, src[:own],
                        {k: src[own + 4 * i : own + 4 * i + 4] for i, k in enumerate(steps)})
    if first:
        scales = [
            pltpu.make_async_copy(scale_s, here_s, scale_sem.at[0]),
            pltpu.make_async_copy(scale_t, here_t, scale_sem.at[1]),
        ]
        for c in scales:
            c.start()
    for c in copies:
        c.start()
    each(lambda c: c.start())
    if first:
        for c in scales:
            c.wait()
        for c in range(column.shape[0] // LANES):
            column[pl.ds(c * LANES, LANES), :] = column_of(here_t[pl.ds(c, 1), :])
        for c in range(lane.shape[1] // LANES):
            lane[:, pl.ds(c * LANES, LANES)] = jnp.broadcast_to(here_s[pl.ds(c, 1), :], (8, LANES))
    for c in copies:
        c.wait()
    each(lambda c: c.wait())


def score_kernel(depth, *refs):
    late = refs[:4]
    tgt_buf, _, column, lane, src_buf, sim, fwd, bwd, one, two, state, src_sem = refs[4:]
    t = lax.axis_index("tgt")
    core, z = t % 2, t // 2
    sources, targets = src_buf.shape[1], tgt_buf.shape[1]
    each = piece_copies(z, core, depth, src_buf, src_sem, (), {depth - 1: late})
    each(lambda c: c.start())
    each(lambda c: c.wait())
    rows = one.shape[0]
    groups, count = sources // GROUP, targets // rows

    def dot(g, r, out):
        out[...] = lax.dot_general(
            tgt_buf[:, pl.ds(pl.multiple_of(r * rows, rows), rows)],
            src_buf[:, pl.ds(pl.multiple_of(g * GROUP, GROUP), GROUP)],
            (((0,), (0,)), ((), ())), preferred_element_type=jnp.float32)

    def write(k, c, row):
        fwd[k, pl.ds(c, 1), :] = row

    def write_rows(k, c, row):
        bwd[k, pl.ds(c, 1), :] = row

    dot(0, 0, one)
    for g in range(groups):

        def body(q, lists, g=g):
            for h, (now, later) in enumerate(((one, two), (two, one))):
                r = 2 * q + h
                base = pl.multiple_of(r * rows, rows)
                if h == 0:
                    dot(g, r + 1, later)
                else:
                    last = r + 1 == count
                    dot(jnp.where(last, min(g + 1, groups - 1), g), jnp.where(last, 0, r + 1), later)

                def load(row, b, now=now, base=base):
                    cols = pl.ds(g * GROUP + LANES * b, LANES)
                    at = pl.ds(base + row, 8)
                    v = now[row : row + 8, LANES * b : LANES * (b + 1)] * lane[:, cols] * column[at, :]
                    sim[at, cols] = v
                    return v

                lists = sweep_block(load, base, rows, g == 0, lists, state)
            return lists

        loop_lists(count // 2, body, write, g)
    finish_rows(targets, write_rows, state)


def margin_kernel(sim, fwd_mine, fwd_other, bwd_all, fwd, bwd, column, lane, state):
    targets, sources = sim.shape
    f = merge4([fwd_mine[k] for k in range(TOP)], [fwd_other[k] for k in range(TOP)])
    f = 0.5 * (0.25 * (f[0] + f[1] + f[2] + f[3]))
    b = 0.5 * (0.25 * (bwd_all[0] + bwd_all[1] + bwd_all[2] + bwd_all[3]))
    for c in range(targets // LANES):
        column[pl.ds(c * LANES, LANES), :] = column_of(b[c : c + 1, :])
    for c in range(sources // LANES):
        lane[:, pl.ds(c * LANES, LANES)] = jnp.broadcast_to(f[c : c + 1, :], (8, LANES))
    rows = math.gcd(targets, 256)

    def write(k, c, row):
        fwd[k, pl.ds(c, 1), :] = row

    def write_rows(k, c, row):
        bwd[k, pl.ds(c, 1), :] = row

    for g in range(sources // GROUP):

        def body(q, lists, g=g):
            base = pl.multiple_of(q * rows, rows)

            def load(row, b):
                at, cols = pl.ds(base + row, 8), pl.ds(g * GROUP + LANES * b, LANES)
                return sim[at, cols] / (lane[:, cols] + column[at, :])

            return sweep_block(load, base, rows, g == 0, lists, state)

        loop_lists(targets // rows, body, write, g)
    finish_rows(targets, write_rows, state)


def merge_kernel(mine, rec, out):
    merged = merge4([mine[k] for k in range(TOP)], [rec[k] for k in range(TOP)])
    for k in range(TOP):
        out[k] = merged[k]


def final_kernel(fwd_mine, fwd_other, bwd_all, forward, backward):
    f = merge4([fwd_mine[k] for k in range(TOP)], [fwd_other[k] for k in range(TOP)])
    for k in range(TOP):
        for c in range(forward.shape[1] // LANES):
            forward[pl.ds(k, 1), pl.ds(c * LANES, LANES)] = f[k][c : c + 1, :]
        for c in range(backward.shape[1] // LANES):
            backward[pl.ds(k, 1), pl.ds(c * LANES, LANES)] = bwd_all[k, pl.ds(c, 1), :]


def f32(*shape):
    return jax.ShapeDtypeStruct(shape, jnp.float32)


def cost(flops, moved):
    return pl.CostEstimate(flops=flops, bytes_accessed=moved, transcendentals=0)


def solution(mesh):
    n_src, n_tgt = mesh.shape["src"], mesh.shape["tgt"]
    depth = n_tgt // 2
    src_bits, z_bits = n_src.bit_length() - 1, depth.bit_length() - 1
    both = ("src", "tgt")

    def flat(s, t):
        return s * n_tgt + t

    devices = [(s, t) for s in range(n_src) for t in range(n_tgt)]
    partner = [(t, t ^ 1) for t in range(n_tgt)]

    def swap(x):
        return lax.ppermute(x, "tgt", partner)

    def along_z(x, step):
        pairs = []
        for t in range(n_tgt):
            z, core = t // 2, t % 2
            if core == 0 and z >= step - 1 and z + 1 < depth:
                pairs.append((t, t + 2))
            if core == 1 and z <= depth - step and z >= 1:
                pairs.append((t, t - 2))
        return lax.ppermute(x, "tgt", pairs)

    def src_masks(step):
        return 1 << step, 1 << (src_bits - 1 - step)

    def along_src(x, masks):
        pairs = [(flat(s, t), flat(s ^ masks[t % 2], t)) for s, t in devices]
        return lax.ppermute(x, both, pairs)

    def merged(mine, rec):
        return pl.pallas_call(
            merge_kernel, out_shape=f32(*mine.shape), in_specs=[VMEM] * 2, out_specs=VMEM,
            compiler_params=params(1), name="merge")(mine, rec)

    def reduce_lists(fwd, bwd):
        for step in range(max(src_bits, z_bits)):
            if step < z_bits:
                pairs = [(t, t ^ (2 << step)) for t in range(n_tgt)]
                from_z = lax.ppermute(fwd, "tgt", pairs)
            if step < src_bits:
                pairs = [(s, s ^ (1 << step)) for s in range(n_src)]
                from_src = lax.ppermute(bwd, "src", pairs)
            if step < z_bits:
                fwd = merged(fwd, from_z)
            if step < src_bits:
                bwd = merged(bwd, from_src)
        return fwd, swap(fwd), bwd

    def compute(src_codes, src_scale, tgt_codes, tgt_scale):
        sources, targets = src_codes.shape[1], tgt_codes.shape[1]
        total = src_codes.shape[0] * n_tgt
        ns, nt = sources // LANES, targets // LANES
        scale_s, scale_t = src_scale.reshape(-1, LANES), tgt_scale.reshape(-1, LANES)

        u, v = src_codes, swap(src_codes)
        own, passed = [u, v], {}
        for step in range(1, depth):
            u = along_z(u, step)
            v = along_z(v, step)
            passed[step] = [u, v, swap(u), swap(v)]

        held = [(tgt_codes, (0, 0))]
        for step in range(src_bits):
            masks = src_masks(step)
            new = []
            for x, m in held:
                new.append((along_src(x, masks), (m[0] ^ masks[0], m[1] ^ masks[1])))
            held = held + new

        def prep(tgt, steps, extra, first):
            src = (own if first else []) + [x for k in steps for x in passed[k]]
            shapes = [jax.ShapeDtypeStruct((total, targets), tgt_codes.dtype),
                      jax.ShapeDtypeStruct((total, sources), src_codes.dtype)]
            sems = [pltpu.SemaphoreType.DMA((len(tgt),)), pltpu.SemaphoreType.DMA((max(len(src), 1),))]
            if first:
                shapes += [f32(targets, LANES), f32(8, sources)]
                sems = [pltpu.VMEM(scale_s.shape, jnp.float32), pltpu.VMEM(scale_t.shape, jnp.float32)] + sems + [
                    pltpu.SemaphoreType.DMA((2,))]
            count = len(tgt) + len(src)
            return pl.pallas_call(
                functools.partial(prep_kernel, [m for _, m in tgt], depth, steps, first, (len(tgt), len(src))),
                out_shape=shapes, in_specs=[ANY] * count + [ANY if first else VMEM] * 2,
                out_specs=[VMEM] * len(shapes), scratch_shapes=sems,
                input_output_aliases={} if first else {count: 0, count + 1: 1},
                compiler_params=params(2), cost_estimate=cost(0, 4 * total * targets))(*[x for x, _ in tgt], *src, *extra)

        steps = list(range(1, depth - 1))
        tgt_block, src_block, column, lane = prep(held[:1], steps[:-1], (scale_s, scale_t), True)
        tgt_block, src_block = prep(held[1:], steps[-1:], (tgt_block, src_block), False)
        block = min(512, targets // 2)
        _, sim, fwd, bwd = pl.pallas_call(
            functools.partial(score_kernel, depth),
            out_shape=(jax.ShapeDtypeStruct((total, sources), src_codes.dtype),
                       f32(targets, sources), f32(TOP, ns, LANES), f32(TOP, nt, LANES)),
            in_specs=[ANY] * 4 + [VMEM] * 4, out_specs=(VMEM,) * 4,
            input_output_aliases={5: 0},
            scratch_shapes=[
                pltpu.VMEM((block, GROUP), jnp.float32),
                pltpu.VMEM((block, GROUP), jnp.float32),
                pltpu.VMEM((TOP, targets, LANES), jnp.float32),
                pltpu.SemaphoreType.DMA((4,)),
            ],
            compiler_params=params(8), cost_estimate=cost(2 * total * sources * targets, 4 * sources * targets),
            name="score")(*passed[depth - 1], tgt_block, src_block, column, lane)

        fwd, bwd = pl.pallas_call(
            margin_kernel,
            out_shape=(f32(TOP, ns, LANES), f32(TOP, nt, LANES)),
            in_specs=[VMEM] * 4, out_specs=(VMEM,) * 2,
            scratch_shapes=[
                pltpu.VMEM((targets, LANES), jnp.float32),
                pltpu.VMEM((8, sources), jnp.float32),
                pltpu.VMEM((TOP, targets, LANES), jnp.float32),
            ],
            compiler_params=params(8), cost_estimate=cost(30 * sources * targets, 4 * sources * targets),
            name="margin")(sim, *reduce_lists(fwd, bwd))
        return pl.pallas_call(
            final_kernel, out_shape=(f32(TOP, sources), f32(TOP, targets)),
            in_specs=[VMEM] * 3, out_specs=(VMEM,) * 2, compiler_params=params(1),
            name="final")(*reduce_lists(fwd, bwd))

    placed = (P("tgt", "src"), P("src"), P("src", "tgt"), P("tgt"))
    return jax.shard_map(
        compute, mesh=mesh, in_specs=placed, out_specs=(P(None, "src"), P(None, "tgt")), check_vma=False)
```

profile of v0, /device:TPU:0, one launch (start us, length us, event | category | flops | bytes accessed | tf_op | source)
XLA Modules:
  0.0 78.3 jit_solution(17833068528286585707)
XLA Ops:
  1.2 4.5 %collective-permute-start = (bf16[128,1536]{1,0:T(8,128)(2,1)}, bf16[128,1536]{1,0:T(8,128)(2,1)S(1)}, u32[]{:S(2)}, u32[]{:S(2)}) collective-permute-start(bf16[128,1536]{1,0:T(8,128)(2,1)} %refs_1_.1), channel_id=1, source_target_pairs={{0,2},{2,4},{3,1},{4,6},{5,3},{7,5},{8,10},{10,12},{11,9},{12,14},... | collective-permute-start | bytes 1179656 | tf_op jit(solution)/shard_map/ppermute | solution.py:302
  5.7 3.5 %collective-permute-start.4 = (bf16[128,1536]{1,0:T(8,128)(2,1)S(1)}, bf16[128,1536]{1,0:T(8,128)(2,1)S(1)}, u32[]{:S(2)}, u32[]{:S(2)}) collective-permute-start(bf16[128,1536]{1,0:T(8,128)(2,1)S(1)} %collective-permute-done.3.refs_2_), channel_id=1, source_target_pairs={{0,2},{2,4},{3,1},{4,6},{5,3},{7,5},{8,10},{10,12},{11,9},{12,14},... | collective-permute-start | bytes 1179656 | tf_op jit(solution)/shard_map/ppermute | solution.py:302
  9.2 1.6 %collective-permute-start.9 = (bf16[256,1024]{1,0:T(8,128)(2,1)}, bf16[256,1024]{1,0:T(8,128)(2,1)S(1)}, u32[]{:S(2)}, u32[]{:S(2)}) collective-permute-start(bf16[256,1024]{1,0:T(8,128)(2,1)} %refs_0_.1), channel_id=1, source_target_pairs={{0,8},{1,17},{2,10},{3,19},{4,12},{5,21},{6,14},{7,23},{8,0},{9,25... | collective-permute-start | bytes 1572872 | tf_op jit(solution)/shard_map/ppermute | solution.py:309
  11.9 3.4 %collective-permute-done.4.refs_4_ = bf16[128,1536]{1,0:T(8,128)(2,1)S(1)} collective-permute-done((bf16[128,1536]{1,0:T(8,128)(2,1)S(1)}, bf16[128,1536]{1,0:T(8,128)(2,1)S(1)}, u32[]{:S(2)}, u32[]{:S(2)}) %collective-permute-start.4) | collective-permute-done | bytes 393248 | tf_op jit(solution)/shard_map/ppermute | solution.py:302
  16.1 1.6 %collective-permute-start.10 = (bf16[256,1024]{1,0:T(8,128)(2,1)}, bf16[256,1024]{1,0:T(8,128)(2,1)S(1)}, u32[]{:S(2)}, u32[]{:S(2)}) collective-permute-start(bf16[256,1024]{1,0:T(8,128)(2,1)} %refs_0_.1), channel_id=1, source_target_pairs={{0,16},{1,9},{2,18},{3,11},{4,20},{5,13},{6,22},{7,15},{8,24},{9,1... | collective-permute-start | bytes 1572872 | tf_op jit(solution)/shard_map/ppermute | solution.py:309
  17.6 0.8 %collective-permute-start.14 = (bf16[128,1536]{1,0:T(8,128)(2,1)S(1)}, bf16[128,1536]{1,0:T(8,128)(2,1)S(1)}, u32[]{:S(2)}, u32[]{:S(2)}) collective-permute-start(bf16[128,1536]{1,0:T(8,128)(2,1)S(1)} %collective-permute-done.refs_3_), channel_id=1, source_target_pairs={{0,1},{1,0},{2,3},{3,2},{4,5},{5,4},{6,7},{7,6},{8,9},{9,8},{10,11... | collective-permute-start | bytes 1179656 | tf_op jit(solution)/shard_map/ppermute | solution.py:292
  19.2 2.5 %collective-permute-start.15 = (bf16[128,1536]{1,0:T(8,128)(2,1)S(1)}, bf16[128,1536]{1,0:T(8,128)(2,1)S(1)}, u32[]{:S(2)}, u32[]{:S(2)}) collective-permute-start(bf16[128,1536]{1,0:T(8,128)(2,1)S(1)} %collective-permute-done.4.refs_4_), channel_id=1, source_target_pairs={{0,1},{1,0},{2,3},{3,2},{4,5},{5,4},{6,7},{7,6},{8,9},{9,8},{10,11... | collective-permute-start | bytes 1179656 | tf_op jit(solution)/shard_map/ppermute | solution.py:292
  22.4 3.1 %collective-permute-done.10.refs_1_ = bf16[256,1024]{1,0:T(8,128)(2,1)S(1)} collective-permute-done((bf16[256,1024]{1,0:T(8,128)(2,1)}, bf16[256,1024]{1,0:T(8,128)(2,1)S(1)}, u32[]{:S(2)}, u32[]{:S(2)}) %collective-permute-start.10) | collective-permute-done | bytes 524320 | tf_op jit(solution)/shard_map/ppermute | solution.py:309
  25.5 1.5 %collective-permute-start.11 = (bf16[256,1024]{1,0:T(8,128)(2,1)S(1)}, bf16[256,1024]{1,0:T(8,128)(2,1)S(1)}, u32[]{:S(2)}, u32[]{:S(2)}) collective-permute-start(bf16[256,1024]{1,0:T(8,128)(2,1)S(1)} %collective-permute-done.9.refs_0_), channel_id=1, source_target_pairs={{0,16},{1,9},{2,18},{3,11},{4,20},{5,13},{6,22},{7,15},{8,24},{9,1... | collective-permute-start | bytes 1572872 | tf_op jit(solution)/shard_map/ppermute | solution.py:309
  27.3 2.6 %collective-permute-start.13 = (bf16[128,1536]{1,0:T(8,128)(2,1)S(1)}, bf16[128,1536]{1,0:T(8,128)(2,1)S(1)}, u32[]{:S(2)}, u32[]{:S(2)}) collective-permute-start(bf16[128,1536]{1,0:T(8,128)(2,1)S(1)} %collective-permute-done.5.refs_4_), channel_id=1, source_target_pairs={{0,1},{1,0},{2,3},{3,2},{4,5},{5,4},{6,7},{7,6},{8,9},{9,8},{10,11... | collective-permute-start | bytes 1179656 | tf_op jit(solution)/shard_map/ppermute | solution.py:292
  29.9 4.2 %collective-permute-start.8 = (bf16[128,1536]{1,0:T(8,128)(2,1)S(1)}, bf16[128,1536]{1,0:T(8,128)(2,1)S(1)}, u32[]{:S(2)}, u32[]{:S(2)}) collective-permute-start(bf16[128,1536]{1,0:T(8,128)(2,1)S(1)} %collective-permute-done.6.refs_1_), channel_id=1, source_target_pairs={{0,1},{1,0},{2,3},{3,2},{4,5},{5,4},{6,7},{7,6},{8,9},{9,8},{10,11... | collective-permute-start | bytes 1179656 | tf_op jit(solution)/shard_map/ppermute | solution.py:292
  34.1 1.0 %copy-done = bf16[256,1024]{1,0:T(8,128)(2,1)S(1)} copy-done((bf16[256,1024]{1,0:T(8,128)(2,1)S(1)}, bf16[256,1024]{1,0:T(8,128)(2,1)}, u32[]{:S(2)}) %copy-start) | copy-done | bytes 524312
  35.2 1.0 %copy-done.1 = bf16[128,1536]{1,0:T(8,128)(2,1)S(1)} copy-done((bf16[128,1536]{1,0:T(8,128)(2,1)S(1)}, bf16[128,1536]{1,0:T(8,128)(2,1)}, u32[]{:S(2)}) %copy-start.1) | copy-done | bytes 393240
  36.2 0.7 copy-done.2
  37.5 1.2 %shard_map.59 = (bf16[1024,1024]{1,0:T(8,128)(2,1)S(1)}, bf16[1024,1536]{1,0:T(8,128)(2,1)S(1)}, f32[1024,128]{1,0:T(8,128)S(1)}, f32[8,1536]{1,0:T(8,128)S(1)}) custom-call(bf16[256,1024]{1,0:T(8,128)(2,1)S(1)} %copy-done, bf16[128,1536]{1,0:T(8,128)(2,1)S(1)} %copy-done.1, bf16[128,1536]{1,0:T(8,128)(2,1)S(1)} %collective-permute-done.3.refs_2_, ...), custom_call_target="tpu_custom_call" | custom-call | bytes 4194304 | tf_op jit(solution)/shard_map/pallas_call | solution.py:361
  39.4 6.3 %score.1 = (bf16[1024,1536]{1,0:T(8,128)(2,1)S(1)}, f32[1024,1536]{1,0:T(8,128)S(1)}, f32[4,12,128]{2,1,0:T(8,128)S(1)}, f32[4,8,128]{2,1,0:T(8,128)S(1)}) custom-call(bf16[128,1536]{1,0:T(8,128)(2,1)S(1)} %collective-permute-done.2.refs_0_, bf16[128,1536]{1,0:T(8,128)(2,1)S(1)} %collective-permute-done.6.refs_1_, ...), custom_call_target="tpu_custom_call", output_to_operand_aliasing={{0}: (5, {})} | custom-call | flops 3221225472 | bytes 6291456 | tf_op jit(solution)/shard_map/score/pallas_call | solution.py:372
  45.7 0.9 %collective-permute-start.16 = (f32[4,12,128]{2,1,0:T(8,128)S(1)}, f32[4,12,128]{2,1,0:T(8,128)S(1)}, u32[]{:S(2)}, u32[]{:S(2)}) collective-permute-start(f32[4,12,128]{2,1,0:T(8,128)S(1)} %get-tuple-element.20.mine), channel_id=1, source_target_pairs={{0,2},{1,3},{2,0},{3,1},{4,6},{5,7},{6,4},{7,5},{8,10},{9,11},{10,... | collective-permute-start | bytes 73736 | tf_op jit(solution)/shard_map/ppermute | solution.py:320
  46.6 3.1 %collective-permute-done.16.rec = f32[4,12,128]{2,1,0:T(8,128)S(1)} collective-permute-done((f32[4,12,128]{2,1,0:T(8,128)S(1)}, f32[4,12,128]{2,1,0:T(8,128)S(1)}, u32[]{:S(2)}, u32[]{:S(2)}) %collective-permute-start.16) | collective-permute-done | bytes 24608 | tf_op jit(solution)/shard_map/ppermute | solution.py:320
  49.7 3.9 %collective-permute-start.17 = (f32[4,12,128]{2,1,0:T(8,128)S(1)}, f32[4,12,128]{2,1,0:T(8,128)S(1)}, u32[]{:S(2)}, u32[]{:S(2)}) collective-permute-start(f32[4,12,128]{2,1,0:T(8,128)S(1)} %merge.8.mine), channel_id=1, source_target_pairs={{0,4},{1,5},{2,6},{3,7},{4,0},{5,1},{6,2},{7,3},{8,12},{9,13},{10,... | collective-permute-start | bytes 73736 | tf_op jit(solution)/shard_map/ppermute | solution.py:320
  53.6 1.5 %collective-permute-start.19 = (f32[4,8,128]{2,1,0:T(8,128)S(1)}, f32[4,8,128]{2,1,0:T(8,128)S(1)}, u32[]{:S(2)}, u32[]{:S(2)}) collective-permute-start(f32[4,8,128]{2,1,0:T(8,128)S(1)} %get-tuple-element.21.mine), channel_id=1, source_target_pairs={{0,8},{8,0},{16,24},{24,16},{1,9},{9,1},{17,25},{25,17},{2,10},{10... | collective-permute-start | bytes 49160 | tf_op jit(solution)/shard_map/ppermute | solution.py:323
  55.0 0.7 collective-permute-done.17.rec
  55.8 1.4 %collective-permute-done.19.rec = f32[4,8,128]{2,1,0:T(8,128)S(1)} collective-permute-done((f32[4,8,128]{2,1,0:T(8,128)S(1)}, f32[4,8,128]{2,1,0:T(8,128)S(1)}, u32[]{:S(2)}, u32[]{:S(2)}) %collective-permute-start.19) | collective-permute-done | bytes 16416 | tf_op jit(solution)/shard_map/ppermute | solution.py:323
  57.3 1.5 %collective-permute-start.20 = (f32[4,8,128]{2,1,0:T(8,128)S(1)}, f32[4,8,128]{2,1,0:T(8,128)S(1)}, u32[]{:S(2)}, u32[]{:S(2)}) collective-permute-start(f32[4,8,128]{2,1,0:T(8,128)S(1)} %merge.10.mine), channel_id=1, source_target_pairs={{0,16},{8,24},{16,0},{24,8},{1,17},{9,25},{17,1},{25,9},{2,18},{10... | collective-permute-start | bytes 49160 | tf_op jit(solution)/shard_map/ppermute | solution.py:323
  58.8 2.2 %collective-permute-done.20.rec = f32[4,8,128]{2,1,0:T(8,128)S(1)} collective-permute-done((f32[4,8,128]{2,1,0:T(8,128)S(1)}, f32[4,8,128]{2,1,0:T(8,128)S(1)}, u32[]{:S(2)}, u32[]{:S(2)}) %collective-permute-start.20) | collective-permute-done | bytes 16416 | tf_op jit(solution)/shard_map/ppermute | solution.py:323
  61.0 3.8 %margin.1 = (f32[4,12,128]{2,1,0:T(8,128)S(1)}, f32[4,8,128]{2,1,0:T(8,128)S(1)}) custom-call(f32[1024,1536]{1,0:T(8,128)S(1)} %get-tuple-element.19.sim, f32[4,12,128]{2,1,0:T(8,128)S(1)} %merge.9.fwd_mine, f32[4,12,128]{2,1,0:T(8,128)S(1)} %collective-permute-done.18.fwd_other, f32[4,8,128]{2,1,0:T(8,128)S(1)} %merge.11.bwd_all), custom_call_target="tpu_custom_call" | custom-call | flops 47185920 | bytes 6291456 | tf_op jit(solution)/shard_map/margin/pallas_call | solution.py:387
  64.8 1.8 %collective-permute-start.21 = (f32[4,12,128]{2,1,0:T(8,128)S(1)}, f32[4,12,128]{2,1,0:T(8,128)S(1)}, u32[]{:S(2)}, u32[]{:S(2)}) collective-permute-start(f32[4,12,128]{2,1,0:T(8,128)S(1)} %get-tuple-element.22.mine), channel_id=1, source_target_pairs={{0,2},{1,3},{2,0},{3,1},{4,6},{5,7},{6,4},{7,5},{8,10},{9,11},{10,... | collective-permute-start | bytes 73736 | tf_op jit(solution)/shard_map/ppermute | solution.py:320
  66.6 2.2 %collective-permute-done.21.rec = f32[4,12,128]{2,1,0:T(8,128)S(1)} collective-permute-done((f32[4,12,128]{2,1,0:T(8,128)S(1)}, f32[4,12,128]{2,1,0:T(8,128)S(1)}, u32[]{:S(2)}, u32[]{:S(2)}) %collective-permute-start.21) | collective-permute-done | bytes 24608 | tf_op jit(solution)/shard_map/ppermute | solution.py:320
  68.8 1.3 %collective-permute-start.22 = (f32[4,12,128]{2,1,0:T(8,128)S(1)}, f32[4,12,128]{2,1,0:T(8,128)S(1)}, u32[]{:S(2)}, u32[]{:S(2)}) collective-permute-start(f32[4,12,128]{2,1,0:T(8,128)S(1)} %merge.12.mine), channel_id=1, source_target_pairs={{0,4},{1,5},{2,6},{3,7},{4,0},{5,1},{6,2},{7,3},{8,12},{9,13},{10,... | collective-permute-start | bytes 73736 | tf_op jit(solution)/shard_map/ppermute | solution.py:320
  70.1 1.5 %collective-permute-start.24 = (f32[4,8,128]{2,1,0:T(8,128)S(1)}, f32[4,8,128]{2,1,0:T(8,128)S(1)}, u32[]{:S(2)}, u32[]{:S(2)}) collective-permute-start(f32[4,8,128]{2,1,0:T(8,128)S(1)} %get-tuple-element.23.mine), channel_id=1, source_target_pairs={{0,8},{8,0},{16,24},{24,16},{1,9},{9,1},{17,25},{25,17},{2,10},{10... | collective-permute-start | bytes 49160 | tf_op jit(solution)/shard_map/ppermute | solution.py:323
  71.6 2.1 %collective-permute-done.22.rec = f32[4,12,128]{2,1,0:T(8,128)S(1)} collective-permute-done((f32[4,12,128]{2,1,0:T(8,128)S(1)}, f32[4,12,128]{2,1,0:T(8,128)S(1)}, u32[]{:S(2)}, u32[]{:S(2)}) %collective-permute-start.22) | collective-permute-done | bytes 24608 | tf_op jit(solution)/shard_map/ppermute | solution.py:320
  73.9 1.5 %collective-permute-start.25 = (f32[4,8,128]{2,1,0:T(8,128)S(1)}, f32[4,8,128]{2,1,0:T(8,128)S(1)}, u32[]{:S(2)}, u32[]{:S(2)}) collective-permute-start(f32[4,8,128]{2,1,0:T(8,128)S(1)} %merge.14.mine), channel_id=1, source_target_pairs={{0,16},{8,24},{16,0},{24,8},{1,17},{9,25},{17,1},{25,9},{2,18},{10... | collective-permute-start | bytes 49160 | tf_op jit(solution)/shard_map/ppermute | solution.py:323
  75.4 2.2 %collective-permute-done.25.rec = f32[4,8,128]{2,1,0:T(8,128)S(1)} collective-permute-done((f32[4,8,128]{2,1,0:T(8,128)S(1)}, f32[4,8,128]{2,1,0:T(8,128)S(1)}, u32[]{:S(2)}, u32[]{:S(2)}) %collective-permute-start.25) | collective-permute-done | bytes 16416 | tf_op jit(solution)/shard_map/ppermute | solution.py:323
  (41 shorter events, 6.3 us)
Async XLA Ops:
  0.6 5.1 %collective-permute-start.3 = (bf16[128,1536]{1,0:T(8,128)(2,1)}, bf16[128,1536]{1,0:T(8,128)(2,1)S(1)}, u32[]{:S(2)}, u32[]{:S(2)}) collective-permute-start(bf16[128,1536]{1,0:T(8,128)(2,1)} %refs_1_.1), channel_id=1, source_target_pairs={{0,1},{1,0},{2,3},{3,2},{4,5},{5,4},{6,7},{7,6},{8,9},{9,8},{10,11... | collective-permute-start | bytes 1179656 | tf_op jit(solution)/shard_map/ppermute | solution.py:292
  1.2 10.1 %collective-permute-start = (bf16[128,1536]{1,0:T(8,128)(2,1)}, bf16[128,1536]{1,0:T(8,128)(2,1)S(1)}, u32[]{:S(2)}, u32[]{:S(2)}) collective-permute-start(bf16[128,1536]{1,0:T(8,128)(2,1)} %refs_1_.1), channel_id=1, source_target_pairs={{0,2},{2,4},{3,1},{4,6},{5,3},{7,5},{8,10},{10,12},{11,9},{12,14},... | collective-permute-start | bytes 1179656 | tf_op jit(solution)/shard_map/ppermute | solution.py:302
  5.7 9.7 %collective-permute-start.4 = (bf16[128,1536]{1,0:T(8,128)(2,1)S(1)}, bf16[128,1536]{1,0:T(8,128)(2,1)S(1)}, u32[]{:S(2)}, u32[]{:S(2)}) collective-permute-start(bf16[128,1536]{1,0:T(8,128)(2,1)S(1)} %collective-permute-done.3.refs_2_), channel_id=1, source_target_pairs={{0,2},{2,4},{3,1},{4,6},{5,3},{7,5},{8,10},{10,12},{11,9},{12,14},... | collective-permute-start | bytes 1179656 | tf_op jit(solution)/shard_map/ppermute | solution.py:302
  9.2 10.0 %collective-permute-start.9 = (bf16[256,1024]{1,0:T(8,128)(2,1)}, bf16[256,1024]{1,0:T(8,128)(2,1)S(1)}, u32[]{:S(2)}, u32[]{:S(2)}) collective-permute-start(bf16[256,1024]{1,0:T(8,128)(2,1)} %refs_0_.1), channel_id=1, source_target_pairs={{0,8},{1,17},{2,10},{3,19},{4,12},{5,21},{6,14},{7,23},{8,0},{9,25... | collective-permute-start | bytes 1572872 | tf_op jit(solution)/shard_map/ppermute | solution.py:309
  11.3 7.2 %collective-permute-start.1 = (bf16[128,1536]{1,0:T(8,128)(2,1)S(1)}, bf16[128,1536]{1,0:T(8,128)(2,1)S(1)}, u32[]{:S(2)}, u32[]{:S(2)}) collective-permute-start(bf16[128,1536]{1,0:T(8,128)(2,1)S(1)} %collective-permute-done.refs_3_), channel_id=1, source_target_pairs={{2,4},{3,1},{4,6},{5,3},{10,12},{11,9},{12,14},{13,11},{18,20},{19... | collective-permute-start | bytes 1179656 | tf_op jit(solution)/shard_map/ppermute | solution.py:302
  15.4 6.3 %collective-permute-start.5 = (bf16[128,1536]{1,0:T(8,128)(2,1)S(1)}, bf16[128,1536]{1,0:T(8,128)(2,1)S(1)}, u32[]{:S(2)}, u32[]{:S(2)}) collective-permute-start(bf16[128,1536]{1,0:T(8,128)(2,1)S(1)} %collective-permute-done.4.refs_4_), channel_id=1, source_target_pairs={{2,4},{3,1},{4,6},{5,3},{10,12},{11,9},{12,14},{13,11},{18,20},{19... | collective-permute-start | bytes 1179656 | tf_op jit(solution)/shard_map/ppermute | solution.py:302
  16.1 9.5 %collective-permute-start.10 = (bf16[256,1024]{1,0:T(8,128)(2,1)}, bf16[256,1024]{1,0:T(8,128)(2,1)S(1)}, u32[]{:S(2)}, u32[]{:S(2)}) collective-permute-start(bf16[256,1024]{1,0:T(8,128)(2,1)} %refs_0_.1), channel_id=1, source_target_pairs={{0,16},{1,9},{2,18},{3,11},{4,20},{5,13},{6,22},{7,15},{8,24},{9,1... | collective-permute-start | bytes 1572872 | tf_op jit(solution)/shard_map/ppermute | solution.py:309
  17.6 9.4 %collective-permute-start.14 = (bf16[128,1536]{1,0:T(8,128)(2,1)S(1)}, bf16[128,1536]{1,0:T(8,128)(2,1)S(1)}, u32[]{:S(2)}, u32[]{:S(2)}) collective-permute-start(bf16[128,1536]{1,0:T(8,128)(2,1)S(1)} %collective-permute-done.refs_3_), channel_id=1, source_target_pairs={{0,1},{1,0},{2,3},{3,2},{4,5},{5,4},{6,7},{7,6},{8,9},{9,8},{10,11... | collective-permute-start | bytes 1179656 | tf_op jit(solution)/shard_map/ppermute | solution.py:292
  18.5 8.8 %collective-permute-start.2 = (bf16[128,1536]{1,0:T(8,128)(2,1)S(1)}, bf16[128,1536]{1,0:T(8,128)(2,1)S(1)}, u32[]{:S(2)}, u32[]{:S(2)}) collective-permute-start(bf16[128,1536]{1,0:T(8,128)(2,1)S(1)} %collective-permute-done.1.refs_3_), channel_id=1, source_target_pairs={{3,1},{4,6},{11,9},{12,14},{19,17},{20,22},{27,25},{28,30}} | collective-permute-start | bytes 1179656 | tf_op jit(solution)/shard_map/ppermute | solution.py:302
  19.2 10.7 %collective-permute-start.15 = (bf16[128,1536]{1,0:T(8,128)(2,1)S(1)}, bf16[128,1536]{1,0:T(8,128)(2,1)S(1)}, u32[]{:S(2)}, u32[]{:S(2)}) collective-permute-start(bf16[128,1536]{1,0:T(8,128)(2,1)S(1)} %collective-permute-done.4.refs_4_), channel_id=1, source_target_pairs={{0,1},{1,0},{2,3},{3,2},{4,5},{5,4},{6,7},{7,6},{8,9},{9,8},{10,11... | collective-permute-start | bytes 1179656 | tf_op jit(solution)/shard_map/ppermute | solution.py:292
  21.7 8.2 %collective-permute-start.6 = (bf16[128,1536]{1,0:T(8,128)(2,1)S(1)}, bf16[128,1536]{1,0:T(8,128)(2,1)S(1)}, u32[]{:S(2)}, u32[]{:S(2)}) collective-permute-start(bf16[128,1536]{1,0:T(8,128)(2,1)S(1)} %collective-permute-done.5.refs_4_), channel_id=1, source_target_pairs={{3,1},{4,6},{11,9},{12,14},{19,17},{20,22},{27,25},{28,30}} | collective-permute-start | bytes 1179656 | tf_op jit(solution)/shard_map/ppermute | solution.py:302
  25.5 13.2 %collective-permute-start.11 = (bf16[256,1024]{1,0:T(8,128)(2,1)S(1)}, bf16[256,1024]{1,0:T(8,128)(2,1)S(1)}, u32[]{:S(2)}, u32[]{:S(2)}) collective-permute-start(bf16[256,1024]{1,0:T(8,128)(2,1)S(1)} %collective-permute-done.9.refs_0_), channel_id=1, source_target_pairs={{0,16},{1,9},{2,18},{3,11},{4,20},{5,13},{6,22},{7,15},{8,24},{9,1... | collective-permute-start | bytes 1572872 | tf_op jit(solution)/shard_map/ppermute | solution.py:309
  27.0 11.7 %collective-permute-start.12 = (bf16[128,1536]{1,0:T(8,128)(2,1)S(1)}, bf16[128,1536]{1,0:T(8,128)(2,1)S(1)}, u32[]{:S(2)}, u32[]{:S(2)}) collective-permute-start(bf16[128,1536]{1,0:T(8,128)(2,1)S(1)} %collective-permute-done.1.refs_3_), channel_id=1, source_target_pairs={{0,1},{1,0},{2,3},{3,2},{4,5},{5,4},{6,7},{7,6},{8,9},{9,8},{10,11... | collective-permute-start | bytes 1179656 | tf_op jit(solution)/shard_map/ppermute | solution.py:292
  27.3 11.4 %collective-permute-start.13 = (bf16[128,1536]{1,0:T(8,128)(2,1)S(1)}, bf16[128,1536]{1,0:T(8,128)(2,1)S(1)}, u32[]{:S(2)}, u32[]{:S(2)}) collective-permute-start(bf16[128,1536]{1,0:T(8,128)(2,1)S(1)} %collective-permute-done.5.refs_4_), channel_id=1, source_target_pairs={{0,1},{1,0},{2,3},{3,2},{4,5},{5,4},{6,7},{7,6},{8,9},{9,8},{10,11... | collective-permute-start | bytes 1179656 | tf_op jit(solution)/shard_map/ppermute | solution.py:292
  29.9 9.5 %collective-permute-start.7 = (bf16[128,1536]{1,0:T(8,128)(2,1)S(1)}, bf16[128,1536]{1,0:T(8,128)(2,1)S(1)}, u32[]{:S(2)}, u32[]{:S(2)}) collective-permute-start(bf16[128,1536]{1,0:T(8,128)(2,1)S(1)} %collective-permute-done.2.refs_0_), channel_id=1, source_target_pairs={{0,1},{1,0},{2,3},{3,2},{4,5},{5,4},{6,7},{7,6},{8,9},{9,8},{10,11... | collective-permute-start | bytes 1179656 | tf_op jit(solution)/shard_map/ppermute | solution.py:292
  29.9 9.5 %collective-permute-start.8 = (bf16[128,1536]{1,0:T(8,128)(2,1)S(1)}, bf16[128,1536]{1,0:T(8,128)(2,1)S(1)}, u32[]{:S(2)}, u32[]{:S(2)}) collective-permute-start(bf16[128,1536]{1,0:T(8,128)(2,1)S(1)} %collective-permute-done.6.refs_1_), channel_id=1, source_target_pairs={{0,1},{1,0},{2,3},{3,2},{4,5},{5,4},{6,7},{7,6},{8,9},{9,8},{10,11... | collective-permute-start | bytes 1179656 | tf_op jit(solution)/shard_map/ppermute | solution.py:292
  34.1 1.0 %copy-start = (bf16[256,1024]{1,0:T(8,128)(2,1)S(1)}, bf16[256,1024]{1,0:T(8,128)(2,1)}, u32[]{:S(2)}) copy-start(bf16[256,1024]{1,0:T(8,128)(2,1)} %refs_0_.1) | copy-start | bytes 1572868
  35.2 1.0 %copy-start.1 = (bf16[128,1536]{1,0:T(8,128)(2,1)S(1)}, bf16[128,1536]{1,0:T(8,128)(2,1)}, u32[]{:S(2)}) copy-start(bf16[128,1536]{1,0:T(8,128)(2,1)} %refs_1_.1) | copy-start | bytes 1179652
  36.2 0.7 copy-start.2
  36.8 0.7 copy-start.3
  45.7 4.0 %collective-permute-start.16 = (f32[4,12,128]{2,1,0:T(8,128)S(1)}, f32[4,12,128]{2,1,0:T(8,128)S(1)}, u32[]{:S(2)}, u32[]{:S(2)}) collective-permute-start(f32[4,12,128]{2,1,0:T(8,128)S(1)} %get-tuple-element.20.mine), channel_id=1, source_target_pairs={{0,2},{1,3},{2,0},{3,1},{4,6},{5,7},{6,4},{7,5},{8,10},{9,11},{10,... | collective-permute-start | bytes 73736 | tf_op jit(solution)/shard_map/ppermute | solution.py:320
  49.7 6.1 %collective-permute-start.17 = (f32[4,12,128]{2,1,0:T(8,128)S(1)}, f32[4,12,128]{2,1,0:T(8,128)S(1)}, u32[]{:S(2)}, u32[]{:S(2)}) collective-permute-start(f32[4,12,128]{2,1,0:T(8,128)S(1)} %merge.8.mine), channel_id=1, source_target_pairs={{0,4},{1,5},{2,6},{3,7},{4,0},{5,1},{6,2},{7,3},{8,12},{9,13},{10,... | collective-permute-start | bytes 73736 | tf_op jit(solution)/shard_map/ppermute | solution.py:320
  53.6 3.7 %collective-permute-start.19 = (f32[4,8,128]{2,1,0:T(8,128)S(1)}, f32[4,8,128]{2,1,0:T(8,128)S(1)}, u32[]{:S(2)}, u32[]{:S(2)}) collective-permute-start(f32[4,8,128]{2,1,0:T(8,128)S(1)} %get-tuple-element.21.mine), channel_id=1, source_target_pairs={{0,8},{8,0},{16,24},{24,16},{1,9},{9,1},{17,25},{25,17},{2,10},{10... | collective-permute-start | bytes 49160 | tf_op jit(solution)/shard_map/ppermute | solution.py:323
  55.8 5.3 %collective-permute-start.18 = (f32[4,12,128]{2,1,0:T(8,128)S(1)}, f32[4,12,128]{2,1,0:T(8,128)S(1)}, u32[]{:S(2)}, u32[]{:S(2)}) collective-permute-start(f32[4,12,128]{2,1,0:T(8,128)S(1)} %merge.9.fwd_mine), channel_id=1, source_target_pairs={{0,1},{1,0},{2,3},{3,2},{4,5},{5,4},{6,7},{7,6},{8,9},{9,8},{10,11... | collective-permute-start | bytes 73736 | tf_op jit(solution)/shard_map/ppermute | solution.py:292
  57.3 3.7 %collective-permute-start.20 = (f32[4,8,128]{2,1,0:T(8,128)S(1)}, f32[4,8,128]{2,1,0:T(8,128)S(1)}, u32[]{:S(2)}, u32[]{:S(2)}) collective-permute-start(f32[4,8,128]{2,1,0:T(8,128)S(1)} %merge.10.mine), channel_id=1, source_target_pairs={{0,16},{8,24},{16,0},{24,8},{1,17},{9,25},{17,1},{25,9},{2,18},{10... | collective-permute-start | bytes 49160 | tf_op jit(solution)/shard_map/ppermute | solution.py:323
  64.8 4.0 %collective-permute-start.21 = (f32[4,12,128]{2,1,0:T(8,128)S(1)}, f32[4,12,128]{2,1,0:T(8,128)S(1)}, u32[]{:S(2)}, u32[]{:S(2)}) collective-permute-start(f32[4,12,128]{2,1,0:T(8,128)S(1)} %get-tuple-element.22.mine), channel_id=1, source_target_pairs={{0,2},{1,3},{2,0},{3,1},{4,6},{5,7},{6,4},{7,5},{8,10},{9,11},{10,... | collective-permute-start | bytes 73736 | tf_op jit(solution)/shard_map/ppermute | solution.py:320
  68.8 4.9 %collective-permute-start.22 = (f32[4,12,128]{2,1,0:T(8,128)S(1)}, f32[4,12,128]{2,1,0:T(8,128)S(1)}, u32[]{:S(2)}, u32[]{:S(2)}) collective-permute-start(f32[4,12,128]{2,1,0:T(8,128)S(1)} %merge.12.mine), channel_id=1, source_target_pairs={{0,4},{1,5},{2,6},{3,7},{4,0},{5,1},{6,2},{7,3},{8,12},{9,13},{10,... | collective-permute-start | bytes 73736 | tf_op jit(solution)/shard_map/ppermute | solution.py:320
  70.1 3.7 %collective-permute-start.24 = (f32[4,8,128]{2,1,0:T(8,128)S(1)}, f32[4,8,128]{2,1,0:T(8,128)S(1)}, u32[]{:S(2)}, u32[]{:S(2)}) collective-permute-start(f32[4,8,128]{2,1,0:T(8,128)S(1)} %get-tuple-element.23.mine), channel_id=1, source_target_pairs={{0,8},{8,0},{16,24},{24,16},{1,9},{9,1},{17,25},{25,17},{2,10},{10... | collective-permute-start | bytes 49160 | tf_op jit(solution)/shard_map/ppermute | solution.py:323
  73.7 3.9 %collective-permute-start.23 = (f32[4,12,128]{2,1,0:T(8,128)S(1)}, f32[4,12,128]{2,1,0:T(8,128)S(1)}, u32[]{:S(2)}, u32[]{:S(2)}) collective-permute-start(f32[4,12,128]{2,1,0:T(8,128)S(1)} %merge.13.fwd_mine), channel_id=1, source_target_pairs={{0,1},{1,0},{2,3},{3,2},{4,5},{5,4},{6,7},{7,6},{8,9},{9,8},{10,11... | collective-permute-start | bytes 73736 | tf_op jit(solution)/shard_map/ppermute | solution.py:292
  73.9 3.7 %collective-permute-start.25 = (f32[4,8,128]{2,1,0:T(8,128)S(1)}, f32[4,8,128]{2,1,0:T(8,128)S(1)}, u32[]{:S(2)}, u32[]{:S(2)}) collective-permute-start(f32[4,8,128]{2,1,0:T(8,128)S(1)} %merge.14.mine), channel_id=1, source_target_pairs={{0,16},{8,24},{16,0},{24,8},{1,17},{9,25},{17,1},{25,9},{2,18},{10... | collective-permute-start | bytes 49160 | tf_op jit(solution)/shard_map/ppermute | solution.py:323
where the time goes:
time: 78.7 us; the launch traced here: 78.3 us
  starting transfers between devices  40.4 us (51%)
  waiting for transfers between devices  21.1 us (27%)
  Pallas kernels  12.6 us (16%)
  local copies, waits for them, and re-layouts  3.42 us (4%)
  between operations  0.81 us (1%)
    ppermute x9, starting transfers between devices, swap(): return lax.ppermute(x, 'tgt', partner)  11.1 us
    ppermute x6, starting transfers between devices, along_z(): return lax.ppermute(x, 'tgt', pairs)  10.7 us
    ppermute x4, waiting for transfers between devices, reduce_lists(): from_z = lax.ppermute(fwd, 'tgt', pairs)  8.04 us
    ppermute x4, starting transfers between devices, reduce_lists(): from_z = lax.ppermute(fwd, 'tgt', pairs)  7.9 us
    pallas_call x1, Pallas kernels, compute(): pl.pallas_call(functools.partial(score_kernel, depth), out_shape=(jax.Sha...  6.3 us
    ppermute x4, starting transfers between devices, reduce_lists(): from_src = lax.ppermute(bwd, 'src', pairs)  5.99 us
    ppermute x4, waiting for transfers between devices, reduce_lists(): from_src = lax.ppermute(bwd, 'src', pairs)  5.98 us
    ppermute x3, starting transfers between devices, along_src(): return lax.ppermute(x, both, pairs)  4.66 us
  transfers between devices with their start and end apart: 26, of which 11 were waited for; matrix products, arithmetic and copies ran while one was open for 0% of the time, Pallas kernels for 2%

commit v1 on v0

--- a/solution.py
+++ b/solution.py
@@ -102,23 +102,20 @@
     return jnp.broadcast_to(row, (LANES, LANES)).T
 
 
-def piece_copies(z, core, depth, buf, sem, own, steps):
+def piece_copies(z, core, depth, buf, sem, entries):
     copies = []
-
-    def copy(piece, block, place):
-        rows = piece.shape[0]
+    for i, (piece, k, j, h, column) in enumerate(entries):
+        rows, width = piece.shape
+        upward = core == j
+        if k == 0:
+            block, place, valid = z, jnp.where(upward, 0, 1), None
+        else:
+            block = jnp.where(upward, z - k, z + k)
+            place = jnp.where(upward, h, 1 - h)
+            valid = jnp.logical_and(block >= 0, block < depth)
         at = pl.multiple_of((block * 2 + place) * rows, rows)
-        return pltpu.make_async_copy(piece, buf.at[pl.ds(at, rows), :], sem.at[len(copies)])
-
-    for place, piece in zip((core, 1 - core), own):
-        copies.append((None, copy(piece, z, place)))
-    for k, four in steps.items():
-        for j in range(2):
-            upward = core == j
-            block = jnp.where(upward, z - k, z + k)
-            valid = jnp.logical_and(block >= 0, block < depth)
-            for h in range(2):
-                copies.append((valid, copy(four[2 * j + h], block, jnp.where(upward, h, 1 - h))))
+        copies.append((valid, pltpu.make_async_copy(
+            piece, buf.at[pl.ds(at, rows), pl.ds(column, width)], sem.at[i])))
 
     def each(act):
         for valid, c in copies:
@@ -130,8 +127,8 @@
     return each
 
 
-def prep_kernel(masks, depth, steps, first, counts, *refs):
-    n, m = counts
+def prep_kernel(masks, depth, places, first, *refs):
+    n, m = len(masks), len(places)
     tgt, src = refs[:n], refs[n : n + m]
     if first:
         scale_s, scale_t, tgt_buf, src_buf, column, lane, here_s, here_t, tgt_sem, src_sem, scale_sem = refs[n + m :]
@@ -145,9 +142,7 @@
         at = jnp.where(core == 0, s ^ masks[i][0], s ^ masks[i][1]) * height
         copies.append(pltpu.make_async_copy(
             tgt[i], tgt_buf.at[pl.ds(pl.multiple_of(at, height), height), :], tgt_sem.at[i]))
-    own = 2 if first else 0
-    each = piece_copies(z, core, depth, src_buf, src_sem, src[:own],
-                        {k: src[own + 4 * i : own + 4 * i + 4] for i, k in enumerate(steps)})
+    each = piece_copies(z, core, depth, src_buf, src_sem, [(x, *at) for x, at in zip(src, places)])
     if first:
         scales = [
             pltpu.make_async_copy(scale_s, here_s, scale_sem.at[0]),
@@ -170,59 +165,67 @@
     each(lambda c: c.wait())
 
 
-def score_kernel(depth, *refs):
-    late = refs[:4]
-    tgt_buf, _, column, lane, src_buf, sim, fwd, bwd, one, two, state, src_sem = refs[4:]
+def score_kernel(depth, places, base, last, *refs):
+    n = len(places)
+    late = refs[:n]
+    if last:
+        (tgt_buf, _, column, lane, fwd_before, _, src_buf, state, sim, fwd, bwd, one, two, src_sem) = refs[n:]
+    else:
+        (tgt_buf, _, column, lane, src_buf, state, sim, fwd, one, two, src_sem) = refs[n:]
     t = lax.axis_index("tgt")
     core, z = t % 2, t // 2
-    sources, targets = src_buf.shape[1], tgt_buf.shape[1]
-    each = piece_copies(z, core, depth, src_buf, src_sem, (), {depth - 1: late})
+    targets = tgt_buf.shape[1]
+    each = piece_copies(z, core, depth, src_buf, src_sem, [(x, *at) for x, at in zip(late, places)])
     each(lambda c: c.start())
     each(lambda c: c.wait())
     rows = one.shape[0]
-    groups, count = sources // GROUP, targets // rows
+    groups = sim.shape[1] // GROUP
+    blocks = [(g, r) for g in range(groups) for r in range(targets // rows)]
 
     def dot(g, r, out):
         out[...] = lax.dot_general(
-            tgt_buf[:, pl.ds(pl.multiple_of(r * rows, rows), rows)],
-            src_buf[:, pl.ds(pl.multiple_of(g * GROUP, GROUP), GROUP)],
+            tgt_buf[:, pl.ds(r * rows, rows)], src_buf[:, pl.ds(base + g * GROUP, GROUP)],
             (((0,), (0,)), ((), ())), preferred_element_type=jnp.float32)
 
-    def write(k, c, row):
-        fwd[k, pl.ds(c, 1), :] = row
+    if last:
+        before = fwd_before.shape[1]
+        fwd[:, :before, :] = fwd_before[...]
+    else:
+        before = 0
 
     def write_rows(k, c, row):
         bwd[k, pl.ds(c, 1), :] = row
 
-    dot(0, 0, one)
-    for g in range(groups):
-
-        def body(q, lists, g=g):
-            for h, (now, later) in enumerate(((one, two), (two, one))):
-                r = 2 * q + h
-                base = pl.multiple_of(r * rows, rows)
-                if h == 0:
-                    dot(g, r + 1, later)
-                else:
-                    last = r + 1 == count
-                    dot(jnp.where(last, min(g + 1, groups - 1), g), jnp.where(last, 0, r + 1), later)
-
-                def load(row, b, now=now, base=base):
-                    cols = pl.ds(g * GROUP + LANES * b, LANES)
-                    at = pl.ds(base + row, 8)
-                    v = now[row : row + 8, LANES * b : LANES * (b + 1)] * lane[:, cols] * column[at, :]
-                    sim[at, cols] = v
-                    return v
-
-                lists = sweep_block(load, base, rows, g == 0, lists, state)
-            return lists
-
-        loop_lists(count // 2, body, write, g)
-    finish_rows(targets, write_rows, state)
-
-
-def margin_kernel(sim, fwd_mine, fwd_other, bwd_all, fwd, bwd, column, lane, state):
-    targets, sources = sim.shape
+    dot(*blocks[0], one)
+    lists = None
+    for i, (g, r) in enumerate(blocks):
+        now, later = (one, two) if i % 2 == 0 else (two, one)
+        if i + 1 < len(blocks):
+            dot(*blocks[i + 1], later)
+
+        def load(row, b, now=now, g=g, r=r):
+            at, out = pl.ds(r * rows + row, 8), pl.ds(g * GROUP + LANES * b, LANES)
+            v = now[row : row + 8, LANES * b : LANES * (b + 1)]
+            v = v * lane[:, pl.ds(base + g * GROUP + LANES * b, LANES)] * column[at, :]
+            sim[at, out] = v
+            return v
+
+        if r == 0:
+            lists = [[jnp.full((8, LANES), -jnp.inf, jnp.float32)] * TOP for _ in range(4)]
+        lists = sweep_block(load, r * rows, rows, g == 0 and not last, lists, state)
+        if r * rows + rows == targets:
+            for b in range(4):
+                best = over_sublanes(lists[b])
+                for k in range(TOP):
+                    fwd[k, pl.ds(before + g * 4 + b, 1), :] = best[k][0:1, :]
+    if last:
+        finish_rows(targets, write_rows, state)
+
+
+def margin_kernel(nsim, *refs):
+    sims = refs[:nsim]
+    fwd_mine, fwd_other, bwd_all, fwd, bwd, column, lane, state = refs[nsim:]
+    targets, sources = sims[0].shape[0], sum(x.shape[1] for x in sims)
     f = merge4([fwd_mine[k] for k in range(TOP)], [fwd_other[k] for k in range(TOP)])
     f = 0.5 * (0.25 * (f[0] + f[1] + f[2] + f[3]))
     b = 0.5 * (0.25 * (bwd_all[0] + bwd_all[1] + bwd_all[2] + bwd_all[3]))
@@ -238,14 +241,15 @@
     def write_rows(k, c, row):
         bwd[k, pl.ds(c, 1), :] = row
 
-    for g in range(sources // GROUP):
-
-        def body(q, lists, g=g):
+    places = [(x, c) for x in sims for c in range(0, x.shape[1], GROUP)]
+    for g, (sim, start) in enumerate(places):
+
+        def body(q, lists, g=g, sim=sim, start=start):
             base = pl.multiple_of(q * rows, rows)
 
             def load(row, b):
                 at, cols = pl.ds(base + row, 8), pl.ds(g * GROUP + LANES * b, LANES)
-                return sim[at, cols] / (lane[:, cols] + column[at, :])
+                return sim[at, pl.ds(start + LANES * b, LANES)] / (lane[:, cols] + column[at, :])
 
             return sweep_block(load, base, rows, g == 0, lists, state)
 
@@ -266,6 +270,10 @@
             forward[pl.ds(k, 1), pl.ds(c * LANES, LANES)] = f[k][c : c + 1, :]
         for c in range(backward.shape[1] // LANES):
             backward[pl.ds(k, 1), pl.ds(c * LANES, LANES)] = bwd_all[k, pl.ds(c, 1), :]
+
+
+def in_hbm(x):
+    return pltpu.with_memory_space_constraint(x, pltpu.HBM)
 
 
 def f32(*shape):
@@ -334,11 +342,19 @@
         scale_s, scale_t = src_scale.reshape(-1, LANES), tgt_scale.reshape(-1, LANES)
 
         u, v = src_codes, swap(src_codes)
-        own, passed = [u, v], {}
+        own = [(u, (0, 0, 0, 0)), (v, (0, 1, 0, 0))]
+        passed, late = [], []
         for step in range(1, depth):
             u = along_z(u, step)
-            v = along_z(v, step)
-            passed[step] = [u, v, swap(u), swap(v)]
+            pair = [(u, (step, 0, 0, 0)), (swap(u), (step, 1, 0, 0))]
+            if step + 1 < depth:
+                v = along_z(v, step)
+                passed += pair + [(v, (step, 0, 1, 0)), (swap(v), (step, 1, 1, 0))]
+            else:
+                for start, stop in ((0, GROUP), (GROUP, sources)):
+                    part = along_z(v[:, start:stop], step)
+                    pair += [(part, (step, 0, 1, start)), (swap(part), (step, 1, 1, start))]
+                late = [pair[:4], pair[4:]]
 
         held = [(tgt_codes, (0, 0))]
         for step in range(src_bits):
@@ -348,53 +364,59 @@
                 new.append((along_src(x, masks), (m[0] ^ masks[0], m[1] ^ masks[1])))
             held = held + new
 
-        def prep(tgt, steps, extra, first):
-            src = (own if first else []) + [x for k in steps for x in passed[k]]
+        def prep(tgt, src, extra, first):
             shapes = [jax.ShapeDtypeStruct((total, targets), tgt_codes.dtype),
                       jax.ShapeDtypeStruct((total, sources), src_codes.dtype)]
-            sems = [pltpu.SemaphoreType.DMA((len(tgt),)), pltpu.SemaphoreType.DMA((max(len(src), 1),))]
+            sems = [pltpu.SemaphoreType.DMA((len(tgt),)), pltpu.SemaphoreType.DMA((len(src),))]
             if first:
                 shapes += [f32(targets, LANES), f32(8, sources)]
                 sems = [pltpu.VMEM(scale_s.shape, jnp.float32), pltpu.VMEM(scale_t.shape, jnp.float32)] + sems + [
                     pltpu.SemaphoreType.DMA((2,))]
             count = len(tgt) + len(src)
             return pl.pallas_call(
-                functools.partial(prep_kernel, [m for _, m in tgt], depth, steps, first, (len(tgt), len(src))),
+                functools.partial(prep_kernel, [m for _, m in tgt], depth, [at for _, at in src], first),
                 out_shape=shapes, in_specs=[ANY] * count + [ANY if first else VMEM] * 2,
                 out_specs=[VMEM] * len(shapes), scratch_shapes=sems,
                 input_output_aliases={} if first else {count: 0, count + 1: 1},
-                compiler_params=params(2), cost_estimate=cost(0, 4 * total * targets))(*[x for x, _ in tgt], *src, *extra)
-
-        steps = list(range(1, depth - 1))
-        tgt_block, src_block, column, lane = prep(held[:1], steps[:-1], (scale_s, scale_t), True)
-        tgt_block, src_block = prep(held[1:], steps[-1:], (tgt_block, src_block), False)
+                compiler_params=params(2), cost_estimate=cost(0, 4 * total * targets))(*[x for x, _ in tgt], *[x for x, _ in src], *extra)
+
+        tgt_block, src_block, column, lane = prep(
+            [(in_hbm(tgt_codes), (0, 0))], [(in_hbm(src_codes), own[0][1]), own[1]],
+            (in_hbm(scale_s), in_hbm(scale_t)), True)
+        tgt_block, src_block = prep(held[1:], passed, (tgt_block, src_block), False)
+
         block = min(512, targets // 2)
-        _, sim, fwd, bwd = pl.pallas_call(
-            functools.partial(score_kernel, depth),
-            out_shape=(jax.ShapeDtypeStruct((total, sources), src_codes.dtype),
-                       f32(targets, sources), f32(TOP, ns, LANES), f32(TOP, nt, LANES)),
-            in_specs=[ANY] * 4 + [VMEM] * 4, out_specs=(VMEM,) * 4,
-            input_output_aliases={5: 0},
-            scratch_shapes=[
-                pltpu.VMEM((block, GROUP), jnp.float32),
-                pltpu.VMEM((block, GROUP), jnp.float32),
-                pltpu.VMEM((TOP, targets, LANES), jnp.float32),
-                pltpu.SemaphoreType.DMA((4,)),
-            ],
-            compiler_params=params(8), cost_estimate=cost(2 * total * sources * targets, 4 * sources * targets),
-            name="score")(*passed[depth - 1], tgt_block, src_block, column, lane)
+        scratch = [pltpu.VMEM((block, GROUP), jnp.float32)] * 2 + [pltpu.SemaphoreType.DMA((4,))]
+        buffers = (jax.ShapeDtypeStruct((total, sources), src_codes.dtype), f32(TOP, targets, LANES))
+
+        def score(pieces, base, width, extra, out):
+            n, last = len(pieces), bool(extra)
+            return pl.pallas_call(
+                functools.partial(score_kernel, depth, [at for _, at in pieces], base, last),
+                out_shape=buffers + (f32(targets, width),) + out,
+                in_specs=[ANY] * n + [VMEM] * (4 + len(extra)), out_specs=(VMEM,) * (3 + len(out)),
+                input_output_aliases={n + 1: 0, n + 5: 1} if last else {n + 1: 0},
+                scratch_shapes=scratch, compiler_params=params(8),
+                cost_estimate=cost(2 * total * width * targets, 4 * width * targets))(
+                    *[x for x, _ in pieces], tgt_block, src_block, column, lane, *extra)
+
+        src_block, state, sim_one, fwd = score(
+            late[0], 0, GROUP, (), (f32(TOP, GROUP // LANES, LANES),))
+        _, _, sim_two, fwd, bwd = score(
+            late[1], GROUP, sources - GROUP, (fwd, state), (f32(TOP, ns, LANES), f32(TOP, nt, LANES)))
+        sims = (sim_one, sim_two)
 
         fwd, bwd = pl.pallas_call(
-            margin_kernel,
+            functools.partial(margin_kernel, len(sims)),
             out_shape=(f32(TOP, ns, LANES), f32(TOP, nt, LANES)),
-            in_specs=[VMEM] * 4, out_specs=(VMEM,) * 2,
+            in_specs=[VMEM] * (len(sims) + 3), out_specs=(VMEM,) * 2,
             scratch_shapes=[
                 pltpu.VMEM((targets, LANES), jnp.float32),
                 pltpu.VMEM((8, sources), jnp.float32),
                 pltpu.VMEM((TOP, targets, LANES), jnp.float32),
             ],
             compiler_params=params(8), cost_estimate=cost(30 * sources * targets, 4 * sources * targets),
-            name="margin")(sim, *reduce_lists(fwd, bwd))
+            name="margin")(*sims, *reduce_lists(fwd, bwd))
         return pl.pallas_call(
             final_kernel, out_shape=(f32(TOP, sources), f32(TOP, targets)),
             in_specs=[VMEM] * 3, out_specs=(VMEM,) * 2, compiler_params=params(1),

time: 78.7 us -> 80.6 us (1.024)
  waiting for transfers between devices: 21.1 us -> 25.9 us
  local copies, waits for them, and re-layouts: 3.42 us -> 0.03 us
    unnamed x8 -> x0, local copies, waits for them, and re-layouts: 3.42 us -> none
    ppermute x3, waiting for transfers between devices: 3.12 us -> 6.41 us  [along_src(): return lax.ppermute(x, both, pairs)]
    ppermute x9 -> x10, starting transfers between devices: 11.1 us -> 14.3 us  [swap(): return lax.ppermute(x, 'tgt', partner)]
    ppermute x4, starting transfers between devices: 7.9 us -> 5.08 us  [reduce_lists(): from_z = lax.ppermute(fwd, 'tgt', pairs)]
    ppermute x4, waiting for transfers between devices: 8.04 us -> 10 us  [reduce_lists(): from_z = lax.ppermute(fwd, 'tgt', pairs)]
    ppermute x4, waiting for transfers between devices: 5.98 us -> 4.91 us  [reduce_lists(): from_src = lax.ppermute(bwd, 'src', pairs)]
    ppermute x3, starting transfers between devices: 4.66 us -> 3.65 us  [along_src(): return lax.ppermute(x, both, pairs)]
    ppermute x6 -> x7, starting transfers between devices: 10.7 us -> 11.3 us  [along_z(): return lax.ppermute(x, 'tgt', pairs)]
  transfers between devices with their start and end apart: 26 -> 28, of which waited for: 11 -> 12; matrix products, arithmetic and copies ran while one was open for 0% -> 0% of each run, Pallas kernels for 2% -> 6%
where the time goes in v1:
time: 80.6 us; the launch traced here: 80.3 us
  starting transfers between devices  40.2 us (50%)
  waiting for transfers between devices  25.9 us (32%)
  Pallas kernels  13.3 us (17%)
  between operations  0.86 us (1%)
    ppermute x10, starting transfers between devices, swap(): return lax.ppermute(x, 'tgt', partner)  14.3 us
    ppermute x7, starting transfers between devices, along_z(): return lax.ppermute(x, 'tgt', pairs)  11.3 us
    ppermute x4, waiting for transfers between devices, reduce_lists(): from_z = lax.ppermute(fwd, 'tgt', pairs)  10 us
    ppermute x3, waiting for transfers between devices, along_src(): return lax.ppermute(x, both, pairs)  6.41 us
    pallas_call x2, Pallas kernels, score(): pl.pallas_call(functools.partial(score_kernel, depth, [at for _, at in pi...  6.33 us
    ppermute x4, starting transfers between devices, reduce_lists(): from_src = lax.ppermute(bwd, 'src', pairs)  5.78 us
    ppermute x4, starting transfers between devices, reduce_lists(): from_z = lax.ppermute(fwd, 'tgt', pairs)  5.08 us
    ppermute x4, waiting for transfers between devices, reduce_lists(): from_src = lax.ppermute(bwd, 'src', pairs)  4.91 us
  transfers between devices with their start and end apart: 28, of which 12 were waited for; matrix products, arithmetic and copies ran while one was open for 0% of the time, Pallas kernels for 6%

profile of v1, /device:TPU:0, one launch (start us, length us, event | category | flops | bytes accessed | tf_op | source)
XLA Modules:
  0.0 80.3 jit_solution(7707699063693181416)
XLA Ops:
  1.2 4.5 %collective-permute-start = (bf16[128,1536]{1,0:T(8,128)(2,1)}, bf16[128,1536]{1,0:T(8,128)(2,1)S(1)}, u32[]{:S(2)}, u32[]{:S(2)}) collective-permute-start(bf16[128,1536]{1,0:T(8,128)(2,1)} %refs_1_.1), channel_id=1, source_target_pairs={{0,2},{2,4},{3,1},{4,6},{5,3},{7,5},{8,10},{10,12},{11,9},{12,14},... | collective-permute-start | bytes 1179656 | tf_op jit(solution)/shard_map/ppermute | solution.py:310
  5.7 1.6 %collective-permute-start.9 = (bf16[256,1024]{1,0:T(8,128)(2,1)}, bf16[256,1024]{1,0:T(8,128)(2,1)S(1)}, u32[]{:S(2)}, u32[]{:S(2)}) collective-permute-start(bf16[256,1024]{1,0:T(8,128)(2,1)} %refs_0_.1), channel_id=1, source_target_pairs={{0,8},{1,17},{2,10},{3,19},{4,12},{5,21},{6,14},{7,23},{8,0},{9,25... | collective-permute-start | bytes 1572872 | tf_op jit(solution)/shard_map/ppermute | solution.py:317
  7.3 3.5 %collective-permute-start.5 = (bf16[128,1536]{1,0:T(8,128)(2,1)S(1)}, bf16[128,1536]{1,0:T(8,128)(2,1)S(1)}, u32[]{:S(2)}, u32[]{:S(2)}) collective-permute-start(bf16[128,1536]{1,0:T(8,128)(2,1)S(1)} %collective-permute-done.4.refs_2_), channel_id=1, source_target_pairs={{0,2},{2,4},{3,1},{4,6},{5,3},{7,5},{8,10},{10,12},{11,9},{12,14},... | collective-permute-start | bytes 1179656 | tf_op jit(solution)/shard_map/ppermute | solution.py:310
  11.3 0.7 collective-permute-start.1
  12.0 4.0 %collective-permute-done.5.refs_5_ = bf16[128,1536]{1,0:T(8,128)(2,1)S(1)} collective-permute-done((bf16[128,1536]{1,0:T(8,128)(2,1)S(1)}, bf16[128,1536]{1,0:T(8,128)(2,1)S(1)}, u32[]{:S(2)}, u32[]{:S(2)}) %collective-permute-start.5) | collective-permute-done | bytes 393248 | tf_op jit(solution)/shard_map/ppermute | solution.py:310
  16.0 0.7 collective-permute-start.6
  16.7 1.6 %collective-permute-start.10 = (bf16[256,1024]{1,0:T(8,128)(2,1)}, bf16[256,1024]{1,0:T(8,128)(2,1)S(1)}, u32[]{:S(2)}, u32[]{:S(2)}) collective-permute-start(bf16[256,1024]{1,0:T(8,128)(2,1)} %refs_0_.1), channel_id=1, source_target_pairs={{0,16},{1,9},{2,18},{3,11},{4,20},{5,13},{6,22},{7,15},{8,24},{9,1... | collective-permute-start | bytes 1572872 | tf_op jit(solution)/shard_map/ppermute | solution.py:317
  18.8 0.7 collective-permute-start.2
  19.5 5.1 %collective-permute-start.14 = (bf16[128,1536]{1,0:T(8,128)(2,1)S(1)}, bf16[128,1536]{1,0:T(8,128)(2,1)S(1)}, u32[]{:S(2)}, u32[]{:S(2)}) collective-permute-start(bf16[128,1536]{1,0:T(8,128)(2,1)S(1)} %collective-permute-done.1.refs_7_), channel_id=1, source_target_pairs={{0,1},{1,0},{2,3},{3,2},{4,5},{5,4},{6,7},{7,6},{8,9},{9,8},{10,11... | collective-permute-start | bytes 1179656 | tf_op jit(solution)/shard_map/ppermute | solution.py:300
  24.6 1.6 %collective-permute-done.10.refs_1_ = bf16[256,1024]{1,0:T(8,128)(2,1)S(1)} collective-permute-done((bf16[256,1024]{1,0:T(8,128)(2,1)}, bf16[256,1024]{1,0:T(8,128)(2,1)S(1)}, u32[]{:S(2)}, u32[]{:S(2)}) %collective-permute-start.10) | collective-permute-done | bytes 524320 | tf_op jit(solution)/shard_map/ppermute | solution.py:317
  26.9 4.9 %collective-permute-done.11.refs_2_ = bf16[256,1024]{1,0:T(8,128)(2,1)S(1)} collective-permute-done((bf16[256,1024]{1,0:T(8,128)(2,1)S(1)}, bf16[256,1024]{1,0:T(8,128)(2,1)S(1)}, u32[]{:S(2)}, u32[]{:S(2)}) %collective-permute-start.11) | collective-permute-done | bytes 524320 | tf_op jit(solution)/shard_map/ppermute | solution.py:317
  32.3 0.7 collective-permute-start.7
  33.0 0.7 collective-permute-start.17
  33.7 7.3 %collective-permute-start.8 = (bf16[128,512]{1,0:T(8,128)(2,1)S(1)}, bf16[128,512]{1,0:T(8,128)(2,1)S(1)}, u32[]{:S(2)}, u32[]{:S(2)}) collective-permute-start(bf16[128,512]{1,0:T(8,128)(2,1)S(1)} %collective-permute-done.7.refs_2_), channel_id=1, source_target_pairs={{0,1},{1,0},{2,3},{3,2},{4,5},{5,4},{6,7},{7,6},{8,9},{9,8},{10,11... | collective-permute-start | bytes 393224 | tf_op jit(solution)/shard_map/ppermute | solution.py:300
  40.9 1.2 %shard_map.59 = (bf16[1024,1024]{1,0:T(8,128)(2,1)S(1)}, bf16[1024,1536]{1,0:T(8,128)(2,1)S(1)}, f32[1024,128]{1,0:T(8,128)S(1)}, f32[8,1536]{1,0:T(8,128)S(1)}) custom-call(bf16[256,1024]{1,0:T(8,128)(2,1)} %refs_0_.1, bf16[128,1536]{1,0:T(8,128)(2,1)} %refs_1_.1, bf16[128,1536]{1,0:T(8,128)(2,1)S(1)} %collective-permute-done.4.refs_2_, f32[12,128]{1,0:T(8,128)} %bitcast.2, ...), custom_call_target="tpu_custom_call" | custom-call | bytes 4194304 | tf_op jit(solution)/shard_map/pallas_call | solution.py:376
  42.2 1.2 %shard_map.60 = (bf16[1024,1024]{1,0:T(8,128)(2,1)S(1)}, bf16[1024,1536]{1,0:T(8,128)(2,1)S(1)}) custom-call(bf16[256,1024]{1,0:T(8,128)(2,1)S(1)} %collective-permute-done.9.refs_0_, bf16[256,1024]{1,0:T(8,128)(2,1)S(1)} %collective-permute-done.10.refs_1_, ...), custom_call_target="tpu_custom_call", output_to_operand_aliasing={{0}: (11, {}), {1}: (12, {})} | custom-call | bytes 4194304 | tf_op jit(solution)/shard_map/pallas_call | solution.py:376
  43.4 2.1 %shard_map.61 = (bf16[1024,1536]{1,0:T(8,128)(2,1)S(1)}, f32[4,1024,128]{2,1,0:T(8,128)S(1)}, f32[1024,512]{1,0:T(8,128)S(1)}, f32[4,4,128]{2,1,0:T(4,128)S(1)}) custom-call(bf16[128,1536]{1,0:T(8,128)(2,1)S(1)} %collective-permute-done.2.refs_0_, bf16[128,1536]{1,0:T(8,128)(2,1)S(1)} %collective-permute-done.3.refs_1_, ...), custom_call_target="tpu_custom_call", output_to_operand_aliasing={{0}: (5, {})} | custom-call | flops 1073741824 | bytes 2097152 | tf_op jit(solution)/shard_map/pallas_call | solution.py:394
  45.5 4.2 %shard_map.62 = (bf16[1024,1536]{1,0:T(8,128)(2,1)S(1)}, f32[4,1024,128]{2,1,0:T(8,128)S(1)}, f32[1024,1024]{1,0:T(8,128)S(1)}, f32[4,12,128]{2,1,0:T(8,128)S(1)}, f32[4,8,128]{2,1,0:T(8,128)S(1)}) custom-call(bf16[128,1024]{1,0:T(8,128)(2,1)S(1)} %collective-permute-done.16.refs_0_, ...), custom_call_target="tpu_custom_call", output_to_operand_aliasing={{0}: (3, {}), {1}: (7, {})} | custom-call | flops 2147483648 | bytes 4194304 | tf_op jit(solution)/shard_map/pallas_call | solution.py:394
  49.9 3.8 %collective-permute-done.18.rec = f32[4,12,128]{2,1,0:T(8,128)S(1)} collective-permute-done((f32[4,12,128]{2,1,0:T(8,128)S(1)}, f32[4,12,128]{2,1,0:T(8,128)S(1)}, u32[]{:S(2)}, u32[]{:S(2)}) %collective-permute-start.18) | collective-permute-done | bytes 24608 | tf_op jit(solution)/shard_map/ppermute | solution.py:328
  53.7 1.5 %collective-permute-start.19 = (f32[4,12,128]{2,1,0:T(8,128)S(1)}, f32[4,12,128]{2,1,0:T(8,128)S(1)}, u32[]{:S(2)}, u32[]{:S(2)}) collective-permute-start(f32[4,12,128]{2,1,0:T(8,128)S(1)} %merge.8.mine), channel_id=1, source_target_pairs={{0,4},{1,5},{2,6},{3,7},{4,0},{5,1},{6,2},{7,3},{8,12},{9,13},{10,... | collective-permute-start | bytes 73736 | tf_op jit(solution)/shard_map/ppermute | solution.py:328
  55.2 1.5 %collective-permute-start.21 = (f32[4,8,128]{2,1,0:T(8,128)S(1)}, f32[4,8,128]{2,1,0:T(8,128)S(1)}, u32[]{:S(2)}, u32[]{:S(2)}) collective-permute-start(f32[4,8,128]{2,1,0:T(8,128)S(1)} %get-tuple-element.29.mine), channel_id=1, source_target_pairs={{0,8},{8,0},{16,24},{24,16},{1,9},{9,1},{17,25},{25,17},{2,10},{10... | collective-permute-start | bytes 49160 | tf_op jit(solution)/shard_map/ppermute | solution.py:331
  56.7 2.0 %collective-permute-done.19.rec = f32[4,12,128]{2,1,0:T(8,128)S(1)} collective-permute-done((f32[4,12,128]{2,1,0:T(8,128)S(1)}, f32[4,12,128]{2,1,0:T(8,128)S(1)}, u32[]{:S(2)}, u32[]{:S(2)}) %collective-permute-start.19) | collective-permute-done | bytes 24608 | tf_op jit(solution)/shard_map/ppermute | solution.py:328
  59.0 1.5 %collective-permute-start.22 = (f32[4,8,128]{2,1,0:T(8,128)S(1)}, f32[4,8,128]{2,1,0:T(8,128)S(1)}, u32[]{:S(2)}, u32[]{:S(2)}) collective-permute-start(f32[4,8,128]{2,1,0:T(8,128)S(1)} %merge.10.mine), channel_id=1, source_target_pairs={{0,16},{8,24},{16,0},{24,8},{1,17},{9,25},{17,1},{25,9},{2,18},{10... | collective-permute-start | bytes 49160 | tf_op jit(solution)/shard_map/ppermute | solution.py:331
  60.5 2.2 %collective-permute-done.22.rec = f32[4,8,128]{2,1,0:T(8,128)S(1)} collective-permute-done((f32[4,8,128]{2,1,0:T(8,128)S(1)}, f32[4,8,128]{2,1,0:T(8,128)S(1)}, u32[]{:S(2)}, u32[]{:S(2)}) %collective-permute-start.22) | collective-permute-done | bytes 16416 | tf_op jit(solution)/shard_map/ppermute | solution.py:331
  62.7 3.9 %margin.1 = (f32[4,12,128]{2,1,0:T(8,128)S(1)}, f32[4,8,128]{2,1,0:T(8,128)S(1)}) custom-call(f32[1024,512]{1,0:T(8,128)S(1)} %get-tuple-element.23.refs_0_, f32[1024,1024]{1,0:T(8,128)S(1)} %get-tuple-element.27.refs_1_, f32[4,12,128]{2,1,0:T(8,128)S(1)} %merge.9.refs_2_, f32[4,12,128]{2,1,0:T(8,128)S(1)} %collective-permute-done.20.refs_3_, ...), custom_call_target="tpu_custom_call" | custom-call | flops 47185920 | bytes 6291456 | tf_op jit(solution)/shard_map/margin/pallas_call | solution.py:409
  66.6 1.9 %collective-permute-start.23 = (f32[4,12,128]{2,1,0:T(8,128)S(1)}, f32[4,12,128]{2,1,0:T(8,128)S(1)}, u32[]{:S(2)}, u32[]{:S(2)}) collective-permute-start(f32[4,12,128]{2,1,0:T(8,128)S(1)} %get-tuple-element.30.mine), channel_id=1, source_target_pairs={{0,2},{1,3},{2,0},{3,1},{4,6},{5,7},{6,4},{7,5},{8,10},{9,11},{10,... | collective-permute-start | bytes 73736 | tf_op jit(solution)/shard_map/ppermute | solution.py:328
  68.5 2.1 %collective-permute-done.23.rec = f32[4,12,128]{2,1,0:T(8,128)S(1)} collective-permute-done((f32[4,12,128]{2,1,0:T(8,128)S(1)}, f32[4,12,128]{2,1,0:T(8,128)S(1)}, u32[]{:S(2)}, u32[]{:S(2)}) %collective-permute-start.23) | collective-permute-done | bytes 24608 | tf_op jit(solution)/shard_map/ppermute | solution.py:328
  70.6 1.6 %collective-permute-start.24 = (f32[4,12,128]{2,1,0:T(8,128)S(1)}, f32[4,12,128]{2,1,0:T(8,128)S(1)}, u32[]{:S(2)}, u32[]{:S(2)}) collective-permute-start(f32[4,12,128]{2,1,0:T(8,128)S(1)} %merge.12.mine), channel_id=1, source_target_pairs={{0,4},{1,5},{2,6},{3,7},{4,0},{5,1},{6,2},{7,3},{8,12},{9,13},{10,... | collective-permute-start | bytes 73736 | tf_op jit(solution)/shard_map/ppermute | solution.py:328
  72.2 1.2 %collective-permute-start.26 = (f32[4,8,128]{2,1,0:T(8,128)S(1)}, f32[4,8,128]{2,1,0:T(8,128)S(1)}, u32[]{:S(2)}, u32[]{:S(2)}) collective-permute-start(f32[4,8,128]{2,1,0:T(8,128)S(1)} %get-tuple-element.31.mine), channel_id=1, source_target_pairs={{0,8},{8,0},{16,24},{24,16},{1,9},{9,1},{17,25},{25,17},{2,10},{10... | collective-permute-start | bytes 49160 | tf_op jit(solution)/shard_map/ppermute | solution.py:331
  73.4 2.1 %collective-permute-done.24.rec = f32[4,12,128]{2,1,0:T(8,128)S(1)} collective-permute-done((f32[4,12,128]{2,1,0:T(8,128)S(1)}, f32[4,12,128]{2,1,0:T(8,128)S(1)}, u32[]{:S(2)}, u32[]{:S(2)}) %collective-permute-start.24) | collective-permute-done | bytes 24608 | tf_op jit(solution)/shard_map/ppermute | solution.py:328
  75.9 1.5 %collective-permute-start.27 = (f32[4,8,128]{2,1,0:T(8,128)S(1)}, f32[4,8,128]{2,1,0:T(8,128)S(1)}, u32[]{:S(2)}, u32[]{:S(2)}) collective-permute-start(f32[4,8,128]{2,1,0:T(8,128)S(1)} %merge.14.mine), channel_id=1, source_target_pairs={{0,16},{8,24},{16,0},{24,8},{1,17},{9,25},{17,1},{25,9},{2,18},{10... | collective-permute-start | bytes 49160 | tf_op jit(solution)/shard_map/ppermute | solution.py:331
  77.4 2.2 %collective-permute-done.27.rec = f32[4,8,128]{2,1,0:T(8,128)S(1)} collective-permute-done((f32[4,8,128]{2,1,0:T(8,128)S(1)}, f32[4,8,128]{2,1,0:T(8,128)S(1)}, u32[]{:S(2)}, u32[]{:S(2)}) %collective-permute-start.27) | collective-permute-done | bytes 16416 | tf_op jit(solution)/shard_map/ppermute | solution.py:331
  (40 shorter events, 4.4 us)
Async XLA Ops:
  0.6 6.6 %collective-permute-start.4 = (bf16[128,1536]{1,0:T(8,128)(2,1)}, bf16[128,1536]{1,0:T(8,128)(2,1)S(1)}, u32[]{:S(2)}, u32[]{:S(2)}) collective-permute-start(bf16[128,1536]{1,0:T(8,128)(2,1)} %refs_1_.1), channel_id=1, source_target_pairs={{0,1},{1,0},{2,3},{3,2},{4,5},{5,4},{6,7},{7,6},{8,9},{9,8},{10,11... | collective-permute-start | bytes 1179656 | tf_op jit(solution)/shard_map/ppermute | solution.py:300
  1.2 10.1 %collective-permute-start = (bf16[128,1536]{1,0:T(8,128)(2,1)}, bf16[128,1536]{1,0:T(8,128)(2,1)S(1)}, u32[]{:S(2)}, u32[]{:S(2)}) collective-permute-start(bf16[128,1536]{1,0:T(8,128)(2,1)} %refs_1_.1), channel_id=1, source_target_pairs={{0,2},{2,4},{3,1},{4,6},{5,3},{7,5},{8,10},{10,12},{11,9},{12,14},... | collective-permute-start | bytes 1179656 | tf_op jit(solution)/shard_map/ppermute | solution.py:310
  5.7 12.6 %collective-permute-start.9 = (bf16[256,1024]{1,0:T(8,128)(2,1)}, bf16[256,1024]{1,0:T(8,128)(2,1)S(1)}, u32[]{:S(2)}, u32[]{:S(2)}) collective-permute-start(bf16[256,1024]{1,0:T(8,128)(2,1)} %refs_0_.1), channel_id=1, source_target_pairs={{0,8},{1,17},{2,10},{3,19},{4,12},{5,21},{6,14},{7,23},{8,0},{9,25... | collective-permute-start | bytes 1572872 | tf_op jit(solution)/shard_map/ppermute | solution.py:317
  7.3 8.7 %collective-permute-start.5 = (bf16[128,1536]{1,0:T(8,128)(2,1)S(1)}, bf16[128,1536]{1,0:T(8,128)(2,1)S(1)}, u32[]{:S(2)}, u32[]{:S(2)}) collective-permute-start(bf16[128,1536]{1,0:T(8,128)(2,1)S(1)} %collective-permute-done.4.refs_2_), channel_id=1, source_target_pairs={{0,2},{2,4},{3,1},{4,6},{5,3},{7,5},{8,10},{10,12},{11,9},{12,14},... | collective-permute-start | bytes 1179656 | tf_op jit(solution)/shard_map/ppermute | solution.py:310
  11.3 7.5 %collective-permute-start.1 = (bf16[128,1536]{1,0:T(8,128)(2,1)S(1)}, bf16[128,1536]{1,0:T(8,128)(2,1)S(1)}, u32[]{:S(2)}, u32[]{:S(2)}) collective-permute-start(bf16[128,1536]{1,0:T(8,128)(2,1)S(1)} %collective-permute-done.refs_3_), channel_id=1, source_target_pairs={{2,4},{3,1},{4,6},{5,3},{10,12},{11,9},{12,14},{13,11},{18,20},{19... | collective-permute-start | bytes 1179656 | tf_op jit(solution)/shard_map/ppermute | solution.py:310
  16.0 3.5 %collective-permute-start.6 = (bf16[128,1536]{1,0:T(8,128)(2,1)S(1)}, bf16[128,1536]{1,0:T(8,128)(2,1)S(1)}, u32[]{:S(2)}, u32[]{:S(2)}) collective-permute-start(bf16[128,1536]{1,0:T(8,128)(2,1)S(1)} %collective-permute-done.5.refs_5_), channel_id=1, source_target_pairs={{2,4},{3,1},{4,6},{5,3},{10,12},{11,9},{12,14},{13,11},{18,20},{19... | collective-permute-start | bytes 1179656 | tf_op jit(solution)/shard_map/ppermute | solution.py:310
  16.7 9.5 %collective-permute-start.10 = (bf16[256,1024]{1,0:T(8,128)(2,1)}, bf16[256,1024]{1,0:T(8,128)(2,1)S(1)}, u32[]{:S(2)}, u32[]{:S(2)}) collective-permute-start(bf16[256,1024]{1,0:T(8,128)(2,1)} %refs_0_.1), channel_id=1, source_target_pairs={{0,16},{1,9},{2,18},{3,11},{4,20},{5,13},{6,22},{7,15},{8,24},{9,1... | collective-permute-start | bytes 1572872 | tf_op jit(solution)/shard_map/ppermute | solution.py:317
  18.3 13.5 %collective-permute-start.11 = (bf16[256,1024]{1,0:T(8,128)(2,1)S(1)}, bf16[256,1024]{1,0:T(8,128)(2,1)S(1)}, u32[]{:S(2)}, u32[]{:S(2)}) collective-permute-start(bf16[256,1024]{1,0:T(8,128)(2,1)S(1)} %collective-permute-done.9.refs_0_), channel_id=1, source_target_pairs={{0,16},{1,9},{2,18},{3,11},{4,20},{5,13},{6,22},{7,15},{8,24},{9,1... | collective-permute-start | bytes 1572872 | tf_op jit(solution)/shard_map/ppermute | solution.py:317
  18.8 8.0 %collective-permute-start.12 = (bf16[128,1536]{1,0:T(8,128)(2,1)S(1)}, bf16[128,1536]{1,0:T(8,128)(2,1)S(1)}, u32[]{:S(2)}, u32[]{:S(2)}) collective-permute-start(bf16[128,1536]{1,0:T(8,128)(2,1)S(1)} %collective-permute-done.refs_3_), channel_id=1, source_target_pairs={{0,1},{1,0},{2,3},{3,2},{4,5},{5,4},{6,7},{7,6},{8,9},{9,8},{10,11... | collective-permute-start | bytes 1179656 | tf_op jit(solution)/shard_map/ppermute | solution.py:300
  18.8 13.0 %collective-permute-start.2 = (bf16[128,1536]{1,0:T(8,128)(2,1)S(1)}, bf16[128,1536]{1,0:T(8,128)(2,1)S(1)}, u32[]{:S(2)}, u32[]{:S(2)}) collective-permute-start(bf16[128,1536]{1,0:T(8,128)(2,1)S(1)} %collective-permute-done.1.refs_7_), channel_id=1, source_target_pairs={{3,1},{4,6},{11,9},{12,14},{19,17},{20,22},{27,25},{28,30}} | collective-permute-start | bytes 1179656 | tf_op jit(solution)/shard_map/ppermute | solution.py:310
  19.5 12.8 %collective-permute-start.14 = (bf16[128,1536]{1,0:T(8,128)(2,1)S(1)}, bf16[128,1536]{1,0:T(8,128)(2,1)S(1)}, u32[]{:S(2)}, u32[]{:S(2)}) collective-permute-start(bf16[128,1536]{1,0:T(8,128)(2,1)S(1)} %collective-permute-done.1.refs_7_), channel_id=1, source_target_pairs={{0,1},{1,0},{2,3},{3,2},{4,5},{5,4},{6,7},{7,6},{8,9},{9,8},{10,11... | collective-permute-start | bytes 1179656 | tf_op jit(solution)/shard_map/ppermute | solution.py:300
  26.1 6.8 %collective-permute-start.16 = (bf16[128,1024]{1,0:T(8,128)(2,1)S(1)}, bf16[128,1024]{1,0:T(8,128)(2,1)S(1)}, u32[]{:S(2)}, u32[]{:S(2)}) collective-permute-start(bf16[128,1024]{1,0:T(8,128)(2,1)S(1)} %slice.9), channel_id=1, source_target_pairs={{3,1},{4,6},{11,9},{12,14},{19,17},{20,22},{27,25},{28,30}} | collective-permute-start | bytes 786440 | tf_op jit(solution)/shard_map/ppermute | solution.py:310
  26.8 15.4 %collective-permute-start.13 = (bf16[128,1536]{1,0:T(8,128)(2,1)S(1)}, bf16[128,1536]{1,0:T(8,128)(2,1)S(1)}, u32[]{:S(2)}, u32[]{:S(2)}) collective-permute-start(bf16[128,1536]{1,0:T(8,128)(2,1)S(1)} %collective-permute-done.5.refs_5_), channel_id=1, source_target_pairs={{0,1},{1,0},{2,3},{3,2},{4,5},{5,4},{6,7},{7,6},{8,9},{9,8},{10,11... | collective-permute-start | bytes 1179656 | tf_op jit(solution)/shard_map/ppermute | solution.py:300
  31.8 10.4 %collective-permute-start.15 = (bf16[128,1536]{1,0:T(8,128)(2,1)S(1)}, bf16[128,1536]{1,0:T(8,128)(2,1)S(1)}, u32[]{:S(2)}, u32[]{:S(2)}) collective-permute-start(bf16[128,1536]{1,0:T(8,128)(2,1)S(1)} %collective-permute-done.6.refs_9_), channel_id=1, source_target_pairs={{0,1},{1,0},{2,3},{3,2},{4,5},{5,4},{6,7},{7,6},{8,9},{9,8},{10,11... | collective-permute-start | bytes 1179656 | tf_op jit(solution)/shard_map/ppermute | solution.py:300
  31.8 11.6 %collective-permute-start.3 = (bf16[128,1536]{1,0:T(8,128)(2,1)S(1)}, bf16[128,1536]{1,0:T(8,128)(2,1)S(1)}, u32[]{:S(2)}, u32[]{:S(2)}) collective-permute-start(bf16[128,1536]{1,0:T(8,128)(2,1)S(1)} %collective-permute-done.2.refs_0_), channel_id=1, source_target_pairs={{0,1},{1,0},{2,3},{3,2},{4,5},{5,4},{6,7},{7,6},{8,9},{9,8},{10,11... | collective-permute-start | bytes 1179656 | tf_op jit(solution)/shard_map/ppermute | solution.py:300
  32.3 1.4 %collective-permute-start.7 = (bf16[128,512]{1,0:T(8,128)(2,1)S(1)}, bf16[128,512]{1,0:T(8,128)(2,1)S(1)}, u32[]{:S(2)}, u32[]{:S(2)}) collective-permute-start(bf16[128,512]{1,0:T(8,128)(2,1)S(1)} %slice.8), channel_id=1, source_target_pairs={{3,1},{4,6},{11,9},{12,14},{19,17},{20,22},{27,25},{28,30}} | collective-permute-start | bytes 393224 | tf_op jit(solution)/shard_map/ppermute | solution.py:310
  33.0 12.6 %collective-permute-start.17 = (bf16[128,1024]{1,0:T(8,128)(2,1)S(1)}, bf16[128,1024]{1,0:T(8,128)(2,1)S(1)}, u32[]{:S(2)}, u32[]{:S(2)}) collective-permute-start(bf16[128,1024]{1,0:T(8,128)(2,1)S(1)} %collective-permute-done.16.refs_0_), channel_id=1, source_target_pairs={{0,1},{1,0},{2,3},{3,2},{4,5},{5,4},{6,7},{7,6},{8,9},{9,8},{10,11... | collective-permute-start | bytes 786440 | tf_op jit(solution)/shard_map/ppermute | solution.py:300
  33.7 9.7 %collective-permute-start.8 = (bf16[128,512]{1,0:T(8,128)(2,1)S(1)}, bf16[128,512]{1,0:T(8,128)(2,1)S(1)}, u32[]{:S(2)}, u32[]{:S(2)}) collective-permute-start(bf16[128,512]{1,0:T(8,128)(2,1)S(1)} %collective-permute-done.7.refs_2_), channel_id=1, source_target_pairs={{0,1},{1,0},{2,3},{3,2},{4,5},{5,4},{6,7},{7,6},{8,9},{9,8},{10,11... | collective-permute-start | bytes 393224 | tf_op jit(solution)/shard_map/ppermute | solution.py:300
  49.8 4.0 %collective-permute-start.18 = (f32[4,12,128]{2,1,0:T(8,128)S(1)}, f32[4,12,128]{2,1,0:T(8,128)S(1)}, u32[]{:S(2)}, u32[]{:S(2)}) collective-permute-start(f32[4,12,128]{2,1,0:T(8,128)S(1)} %get-tuple-element.28.mine), channel_id=1, source_target_pairs={{0,2},{1,3},{2,0},{3,1},{4,6},{5,7},{6,4},{7,5},{8,10},{9,11},{10,... | collective-permute-start | bytes 73736 | tf_op jit(solution)/shard_map/ppermute | solution.py:328
  53.7 5.0 %collective-permute-start.19 = (f32[4,12,128]{2,1,0:T(8,128)S(1)}, f32[4,12,128]{2,1,0:T(8,128)S(1)}, u32[]{:S(2)}, u32[]{:S(2)}) collective-permute-start(f32[4,12,128]{2,1,0:T(8,128)S(1)} %merge.8.mine), channel_id=1, source_target_pairs={{0,4},{1,5},{2,6},{3,7},{4,0},{5,1},{6,2},{7,3},{8,12},{9,13},{10,... | collective-permute-start | bytes 73736 | tf_op jit(solution)/shard_map/ppermute | solution.py:328
  55.2 3.7 %collective-permute-start.21 = (f32[4,8,128]{2,1,0:T(8,128)S(1)}, f32[4,8,128]{2,1,0:T(8,128)S(1)}, u32[]{:S(2)}, u32[]{:S(2)}) collective-permute-start(f32[4,8,128]{2,1,0:T(8,128)S(1)} %get-tuple-element.29.mine), channel_id=1, source_target_pairs={{0,8},{8,0},{16,24},{24,16},{1,9},{9,1},{17,25},{25,17},{2,10},{10... | collective-permute-start | bytes 49160 | tf_op jit(solution)/shard_map/ppermute | solution.py:331
  58.8 4.0 %collective-permute-start.20 = (f32[4,12,128]{2,1,0:T(8,128)S(1)}, f32[4,12,128]{2,1,0:T(8,128)S(1)}, u32[]{:S(2)}, u32[]{:S(2)}) collective-permute-start(f32[4,12,128]{2,1,0:T(8,128)S(1)} %merge.9.refs_2_), channel_id=1, source_target_pairs={{0,1},{1,0},{2,3},{3,2},{4,5},{5,4},{6,7},{7,6},{8,9},{9,8},{10,11... | collective-permute-start | bytes 73736 | tf_op jit(solution)/shard_map/ppermute | solution.py:300
  59.0 3.7 %collective-permute-start.22 = (f32[4,8,128]{2,1,0:T(8,128)S(1)}, f32[4,8,128]{2,1,0:T(8,128)S(1)}, u32[]{:S(2)}, u32[]{:S(2)}) collective-permute-start(f32[4,8,128]{2,1,0:T(8,128)S(1)} %merge.10.mine), channel_id=1, source_target_pairs={{0,16},{8,24},{16,0},{24,8},{1,17},{9,25},{17,1},{25,9},{2,18},{10... | collective-permute-start | bytes 49160 | tf_op jit(solution)/shard_map/ppermute | solution.py:331
  66.6 4.0 %collective-permute-start.23 = (f32[4,12,128]{2,1,0:T(8,128)S(1)}, f32[4,12,128]{2,1,0:T(8,128)S(1)}, u32[]{:S(2)}, u32[]{:S(2)}) collective-permute-start(f32[4,12,128]{2,1,0:T(8,128)S(1)} %get-tuple-element.30.mine), channel_id=1, source_target_pairs={{0,2},{1,3},{2,0},{3,1},{4,6},{5,7},{6,4},{7,5},{8,10},{9,11},{10,... | collective-permute-start | bytes 73736 | tf_op jit(solution)/shard_map/ppermute | solution.py:328
  70.6 4.9 %collective-permute-start.24 = (f32[4,12,128]{2,1,0:T(8,128)S(1)}, f32[4,12,128]{2,1,0:T(8,128)S(1)}, u32[]{:S(2)}, u32[]{:S(2)}) collective-permute-start(f32[4,12,128]{2,1,0:T(8,128)S(1)} %merge.12.mine), channel_id=1, source_target_pairs={{0,4},{1,5},{2,6},{3,7},{4,0},{5,1},{6,2},{7,3},{8,12},{9,13},{10,... | collective-permute-start | bytes 73736 | tf_op jit(solution)/shard_map/ppermute | solution.py:328
  72.2 3.7 %collective-permute-start.26 = (f32[4,8,128]{2,1,0:T(8,128)S(1)}, f32[4,8,128]{2,1,0:T(8,128)S(1)}, u32[]{:S(2)}, u32[]{:S(2)}) collective-permute-start(f32[4,8,128]{2,1,0:T(8,128)S(1)} %get-tuple-element.31.mine), channel_id=1, source_target_pairs={{0,8},{8,0},{16,24},{24,16},{1,9},{9,1},{17,25},{25,17},{2,10},{10... | collective-permute-start | bytes 49160 | tf_op jit(solution)/shard_map/ppermute | solution.py:331
  75.5 4.2 %collective-permute-start.25 = (f32[4,12,128]{2,1,0:T(8,128)S(1)}, f32[4,12,128]{2,1,0:T(8,128)S(1)}, u32[]{:S(2)}, u32[]{:S(2)}) collective-permute-start(f32[4,12,128]{2,1,0:T(8,128)S(1)} %merge.13.fwd_mine), channel_id=1, source_target_pairs={{0,1},{1,0},{2,3},{3,2},{4,5},{5,4},{6,7},{7,6},{8,9},{9,8},{10,11... | collective-permute-start | bytes 73736 | tf_op jit(solution)/shard_map/ppermute | solution.py:300
  75.9 3.7 %collective-permute-start.27 = (f32[4,8,128]{2,1,0:T(8,128)S(1)}, f32[4,8,128]{2,1,0:T(8,128)S(1)}, u32[]{:S(2)}, u32[]{:S(2)}) collective-permute-start(f32[4,8,128]{2,1,0:T(8,128)S(1)} %merge.14.mine), channel_id=1, source_target_pairs={{0,16},{8,24},{16,0},{24,8},{1,17},{9,25},{17,1},{25,9},{2,18},{10... | collective-permute-start | bytes 49160 | tf_op jit(solution)/shard_map/ppermute | solution.py:331

commit v2 on v0

--- a/solution.py
+++ b/solution.py
@@ -268,6 +268,10 @@
             backward[pl.ds(k, 1), pl.ds(c * LANES, LANES)] = bwd_all[k, pl.ds(c, 1), :]
 
 
+def in_hbm(x):
+    return pltpu.with_memory_space_constraint(x, pltpu.HBM)
+
+
 def f32(*shape):
     return jax.ShapeDtypeStruct(shape, jnp.float32)
 
@@ -292,13 +296,14 @@
         return lax.ppermute(x, "tgt", partner)
 
     def along_z(x, step):
+        hop, first = (2, 0) if step == 2 else (1, step - 1)
         pairs = []
         for t in range(n_tgt):
             z, core = t // 2, t % 2
-            if core == 0 and z >= step - 1 and z + 1 < depth:
-                pairs.append((t, t + 2))
-            if core == 1 and z <= depth - step and z >= 1:
-                pairs.append((t, t - 2))
+            if core == 0 and z >= first and z + hop < depth:
+                pairs.append((t, t + 2 * hop))
+            if core == 1 and z < depth - first and z >= hop:
+                pairs.append((t, t - 2 * hop))
         return lax.ppermute(x, "tgt", pairs)
 
     def src_masks(step):
@@ -336,8 +341,8 @@
         u, v = src_codes, swap(src_codes)
         own, passed = [u, v], {}
         for step in range(1, depth):
-            u = along_z(u, step)
-            v = along_z(v, step)
+            u = along_z(own[0] if step == 2 else u, step)
+            v = along_z(own[1] if step == 2 else v, step)
             passed[step] = [u, v, swap(u), swap(v)]
 
         held = [(tgt_codes, (0, 0))]
@@ -350,6 +355,8 @@
 
         def prep(tgt, steps, extra, first):
             src = (own if first else []) + [x for k in steps for x in passed[k]]
+            if first:
+                tgt, src = [(in_hbm(tgt[0][0]), tgt[0][1])], [in_hbm(src[0]), src[1]]
             shapes = [jax.ShapeDtypeStruct((total, targets), tgt_codes.dtype),
                       jax.ShapeDtypeStruct((total, sources), src_codes.dtype)]
             sems = [pltpu.SemaphoreType.DMA((len(tgt),)), pltpu.SemaphoreType.DMA((max(len(src), 1),))]
@@ -366,8 +373,8 @@
                 compiler_params=params(2), cost_estimate=cost(0, 4 * total * targets))(*[x for x, _ in tgt], *src, *extra)
 
         steps = list(range(1, depth - 1))
-        tgt_block, src_block, column, lane = prep(held[:1], steps[:-1], (scale_s, scale_t), True)
-        tgt_block, src_block = prep(held[1:], steps[-1:], (tgt_block, src_block), False)
+        tgt_block, src_block, column, lane = prep(held[:1], [], (in_hbm(scale_s), in_hbm(scale_t)), True)
+        tgt_block, src_block = prep(held[1:], steps, (tgt_block, src_block), False)
         block = min(512, targets // 2)
         _, sim, fwd, bwd = pl.pallas_call(
             functools.partial(score_kernel, depth),

time: 78.7 us -> 82.4 us (1.047)
  starting transfers between devices: 40.4 us -> 48.5 us
  local copies, waits for them, and re-layouts: 3.42 us -> 0 us
  waiting for transfers between devices: 21.1 us -> 19.9 us
    ppermute x6, starting transfers between devices: 10.7 us -> 17 us  [along_z(): return lax.ppermute(x, 'tgt', pairs)]
    unnamed x8 -> x0, local copies, waits for them, and re-layouts: 3.42 us -> none
    ppermute x4, starting transfers between devices: 7.9 us -> 11.1 us  [reduce_lists(): from_z = lax.ppermute(fwd, 'tgt', pairs)]
    ppermute x3, waiting for transfers between devices: 3.12 us -> 0.01 us  [along_src(): return lax.ppermute(x, both, pairs)]
    ppermute x6, waiting for transfers between devices: 3.95 us -> 5.35 us  [along_z(): return lax.ppermute(x, 'tgt', pairs)]
    ppermute x3, starting transfers between devices: 4.66 us -> 3.58 us  [along_src(): return lax.ppermute(x, both, pairs)]
  transfers between devices with their start and end apart: 26 -> 26, of which waited for: 11 -> 10; matrix products, arithmetic and copies ran while one was open for 0% -> 0% of each run, Pallas kernels for 2% -> 3%
where the time goes in v2:
time: 82.4 us; the launch traced here: 82.2 us
  starting transfers between devices  48.5 us (59%)
  waiting for transfers between devices  19.9 us (24%)
  Pallas kernels  12.9 us (16%)
  between operations  0.84 us (1%)
    ppermute x6, starting transfers between devices, along_z(): return lax.ppermute(x, 'tgt', pairs)  17 us
    ppermute x4, starting transfers between devices, reduce_lists(): from_z = lax.ppermute(fwd, 'tgt', pairs)  11.1 us
    ppermute x9, starting transfers between devices, swap(): return lax.ppermute(x, 'tgt', partner)  10.8 us
    ppermute x4, waiting for transfers between devices, reduce_lists(): from_z = lax.ppermute(fwd, 'tgt', pairs)  8.05 us
    ppermute x4, waiting for transfers between devices, reduce_lists(): from_src = lax.ppermute(bwd, 'src', pairs)  6.51 us
    pallas_call x1, Pallas kernels, compute(): pl.pallas_call(functools.partial(score_kernel, depth), out_shape=(jax.Sha...  6.08 us
    ppermute x4, starting transfers between devices, reduce_lists(): from_src = lax.ppermute(bwd, 'src', pairs)  6.01 us
    ppermute x6, waiting for transfers between devices, along_z(): return lax.ppermute(x, 'tgt', pairs)  5.35 us
  transfers between devices with their start and end apart: 26, of which 10 were waited for; matrix products, arithmetic and copies ran while one was open for 0% of the time, Pallas kernels for 3%

profile of v2, /device:TPU:0, one launch (start us, length us, event | category | flops | bytes accessed | tf_op | source)
XLA Modules:
  0.0 82.2 jit_solution(12702953880964978104)
XLA Ops:
  0.6 0.6 collective-permute-start.2
  1.2 5.5 %collective-permute-start = (bf16[128,1536]{1,0:T(8,128)(2,1)}, bf16[128,1536]{1,0:T(8,128)(2,1)S(1)}, u32[]{:S(2)}, u32[]{:S(2)}) collective-permute-start(bf16[128,1536]{1,0:T(8,128)(2,1)} %refs_1_.1), channel_id=1, source_target_pairs={{0,4},{2,6},{5,1},{7,3},{8,12},{10,14},{13,9},{15,11},{16,20},{18,... | collective-permute-start | bytes 1179656 | tf_op jit(solution)/shard_map/ppermute | solution.py:307
  6.7 1.6 %collective-permute-start.7 = (bf16[256,1024]{1,0:T(8,128)(2,1)}, bf16[256,1024]{1,0:T(8,128)(2,1)S(1)}, u32[]{:S(2)}, u32[]{:S(2)}) collective-permute-start(bf16[256,1024]{1,0:T(8,128)(2,1)} %refs_0_.1), channel_id=1, source_target_pairs={{0,8},{1,17},{2,10},{3,19},{4,12},{5,21},{6,14},{7,23},{8,0},{9,25... | collective-permute-start | bytes 1572872 | tf_op jit(solution)/shard_map/ppermute | solution.py:314
  8.3 1.5 %collective-permute-start.8 = (bf16[256,1024]{1,0:T(8,128)(2,1)}, bf16[256,1024]{1,0:T(8,128)(2,1)S(1)}, u32[]{:S(2)}, u32[]{:S(2)}) collective-permute-start(bf16[256,1024]{1,0:T(8,128)(2,1)} %refs_0_.1), channel_id=1, source_target_pairs={{0,16},{1,9},{2,18},{3,11},{4,20},{5,13},{6,22},{7,15},{8,24},{9,1... | collective-permute-start | bytes 1572872 | tf_op jit(solution)/shard_map/ppermute | solution.py:314
  9.8 3.5 %collective-permute-start.10 = (bf16[128,1536]{1,0:T(8,128)(2,1)}, bf16[128,1536]{1,0:T(8,128)(2,1)S(1)}, u32[]{:S(2)}, u32[]{:S(2)}) collective-permute-start(bf16[128,1536]{1,0:T(8,128)(2,1)} %refs_1_.1), channel_id=1, source_target_pairs={{0,2},{2,4},{3,1},{4,6},{5,3},{7,5},{8,10},{10,12},{11,9},{12,14},... | collective-permute-start | bytes 1179656 | tf_op jit(solution)/shard_map/ppermute | solution.py:307
  13.3 1.3 %collective-permute-start.3 = (bf16[128,1536]{1,0:T(8,128)(2,1)S(1)}, bf16[128,1536]{1,0:T(8,128)(2,1)S(1)}, u32[]{:S(2)}, u32[]{:S(2)}) collective-permute-start(bf16[128,1536]{1,0:T(8,128)(2,1)S(1)} %collective-permute-done.2.refs_2_), channel_id=1, source_target_pairs={{0,4},{2,6},{5,1},{7,3},{8,12},{10,14},{13,9},{15,11},{16,20},{18,... | collective-permute-start | bytes 1179656 | tf_op jit(solution)/shard_map/ppermute | solution.py:307
  14.6 5.3 %collective-permute-start.11 = (bf16[128,1536]{1,0:T(8,128)(2,1)S(1)}, bf16[128,1536]{1,0:T(8,128)(2,1)S(1)}, u32[]{:S(2)}, u32[]{:S(2)}) collective-permute-start(bf16[128,1536]{1,0:T(8,128)(2,1)S(1)} %collective-permute-done.2.refs_2_), channel_id=1, source_target_pairs={{0,2},{2,4},{3,1},{4,6},{5,3},{7,5},{8,10},{10,12},{11,9},{12,14},... | collective-permute-start | bytes 1179656 | tf_op jit(solution)/shard_map/ppermute | solution.py:307
  20.5 0.7 collective-permute-start.1
  21.2 1.8 %collective-permute-done.3.refs_8_ = bf16[128,1536]{1,0:T(8,128)(2,1)S(1)} collective-permute-done((bf16[128,1536]{1,0:T(8,128)(2,1)S(1)}, bf16[128,1536]{1,0:T(8,128)(2,1)S(1)}, u32[]{:S(2)}, u32[]{:S(2)}) %collective-permute-start.3) | collective-permute-done | bytes 393248 | tf_op jit(solution)/shard_map/ppermute | solution.py:307
  23.0 0.7 collective-permute-start.4
  23.7 3.5 %collective-permute-done.11.refs_4_ = bf16[128,1536]{1,0:T(8,128)(2,1)S(1)} collective-permute-done((bf16[128,1536]{1,0:T(8,128)(2,1)S(1)}, bf16[128,1536]{1,0:T(8,128)(2,1)S(1)}, u32[]{:S(2)}, u32[]{:S(2)}) %collective-permute-start.11) | collective-permute-done | bytes 393248 | tf_op jit(solution)/shard_map/ppermute | solution.py:307
  27.7 4.1 %collective-permute-start.15 = (bf16[128,1536]{1,0:T(8,128)(2,1)S(1)}, bf16[128,1536]{1,0:T(8,128)(2,1)S(1)}, u32[]{:S(2)}, u32[]{:S(2)}) collective-permute-start(bf16[128,1536]{1,0:T(8,128)(2,1)S(1)} %collective-permute-done.3.refs_8_), channel_id=1, source_target_pairs={{0,1},{1,0},{2,3},{3,2},{4,5},{5,4},{6,7},{7,6},{8,9},{9,8},{10,11... | collective-permute-start | bytes 1179656 | tf_op jit(solution)/shard_map/ppermute | solution.py:296
  32.0 1.4 %collective-permute-start.5 = (bf16[128,1536]{1,0:T(8,128)(2,1)S(1)}, bf16[128,1536]{1,0:T(8,128)(2,1)S(1)}, u32[]{:S(2)}, u32[]{:S(2)}) collective-permute-start(bf16[128,1536]{1,0:T(8,128)(2,1)S(1)} %collective-permute-done.1.refs_0_), channel_id=1, source_target_pairs={{0,1},{1,0},{2,3},{3,2},{4,5},{5,4},{6,7},{7,6},{8,9},{9,8},{10,11... | collective-permute-start | bytes 1179656 | tf_op jit(solution)/shard_map/ppermute | solution.py:296
  33.4 3.9 %collective-permute-start.6 = (bf16[128,1536]{1,0:T(8,128)(2,1)S(1)}, bf16[128,1536]{1,0:T(8,128)(2,1)S(1)}, u32[]{:S(2)}, u32[]{:S(2)}) collective-permute-start(bf16[128,1536]{1,0:T(8,128)(2,1)S(1)} %collective-permute-done.4.refs_1_), channel_id=1, source_target_pairs={{0,1},{1,0},{2,3},{3,2},{4,5},{5,4},{6,7},{7,6},{8,9},{9,8},{10,11... | collective-permute-start | bytes 1179656 | tf_op jit(solution)/shard_map/ppermute | solution.py:296
  37.3 1.2 %shard_map.59 = (bf16[1024,1024]{1,0:T(8,128)(2,1)S(1)}, bf16[1024,1536]{1,0:T(8,128)(2,1)S(1)}, f32[1024,128]{1,0:T(8,128)S(1)}, f32[8,1536]{1,0:T(8,128)S(1)}) custom-call(bf16[256,1024]{1,0:T(8,128)(2,1)} %refs_0_.1, bf16[128,1536]{1,0:T(8,128)(2,1)} %refs_1_.1, bf16[128,1536]{1,0:T(8,128)(2,1)S(1)} %collective-permute-done.2.refs_2_, f32[12,128]{1,0:T(8,128)} %bitcast.2, ...), custom_call_target="tpu_custom_call" | custom-call | bytes 4194304 | tf_op jit(solution)/shard_map/pallas_call | solution.py:368
  38.6 1.2 %shard_map.60 = (bf16[1024,1024]{1,0:T(8,128)(2,1)S(1)}, bf16[1024,1536]{1,0:T(8,128)(2,1)S(1)}) custom-call(bf16[256,1024]{1,0:T(8,128)(2,1)S(1)} %collective-permute-done.7.refs_0_, bf16[256,1024]{1,0:T(8,128)(2,1)S(1)} %collective-permute-done.8.refs_1_, ...), custom_call_target="tpu_custom_call", output_to_operand_aliasing={{0}: (11, {}), {1}: (12, {})} | custom-call | bytes 4194304 | tf_op jit(solution)/shard_map/pallas_call | solution.py:368
  39.8 6.1 %score.1 = (bf16[1024,1536]{1,0:T(8,128)(2,1)S(1)}, f32[1024,1536]{1,0:T(8,128)S(1)}, f32[4,12,128]{2,1,0:T(8,128)S(1)}, f32[4,8,128]{2,1,0:T(8,128)S(1)}) custom-call(bf16[128,1536]{1,0:T(8,128)(2,1)S(1)} %collective-permute-done.1.refs_0_, bf16[128,1536]{1,0:T(8,128)(2,1)S(1)} %collective-permute-done.4.refs_1_, ...), custom_call_target="tpu_custom_call", output_to_operand_aliasing={{0}: (5, {})} | custom-call | flops 3221225472 | bytes 6291456 | tf_op jit(solution)/shard_map/score/pallas_call | solution.py:379
  45.9 5.4 %collective-permute-start.16 = (f32[4,12,128]{2,1,0:T(8,128)S(1)}, f32[4,12,128]{2,1,0:T(8,128)S(1)}, u32[]{:S(2)}, u32[]{:S(2)}) collective-permute-start(f32[4,12,128]{2,1,0:T(8,128)S(1)} %get-tuple-element.20.mine), channel_id=1, source_target_pairs={{0,2},{1,3},{2,0},{3,1},{4,6},{5,7},{6,4},{7,5},{8,10},{9,11},{10,... | collective-permute-start | bytes 73736 | tf_op jit(solution)/shard_map/ppermute | solution.py:325
  51.3 1.9 %collective-permute-done.16.rec = f32[4,12,128]{2,1,0:T(8,128)S(1)} collective-permute-done((f32[4,12,128]{2,1,0:T(8,128)S(1)}, f32[4,12,128]{2,1,0:T(8,128)S(1)}, u32[]{:S(2)}, u32[]{:S(2)}) %collective-permute-start.16) | collective-permute-done | bytes 24608 | tf_op jit(solution)/shard_map/ppermute | solution.py:325
  53.2 4.0 %collective-permute-start.17 = (f32[4,12,128]{2,1,0:T(8,128)S(1)}, f32[4,12,128]{2,1,0:T(8,128)S(1)}, u32[]{:S(2)}, u32[]{:S(2)}) collective-permute-start(f32[4,12,128]{2,1,0:T(8,128)S(1)} %merge.8.mine), channel_id=1, source_target_pairs={{0,4},{1,5},{2,6},{3,7},{4,0},{5,1},{6,2},{7,3},{8,12},{9,13},{10,... | collective-permute-start | bytes 73736 | tf_op jit(solution)/shard_map/ppermute | solution.py:325
  57.3 1.5 %collective-permute-start.19 = (f32[4,8,128]{2,1,0:T(8,128)S(1)}, f32[4,8,128]{2,1,0:T(8,128)S(1)}, u32[]{:S(2)}, u32[]{:S(2)}) collective-permute-start(f32[4,8,128]{2,1,0:T(8,128)S(1)} %get-tuple-element.21.mine), channel_id=1, source_target_pairs={{0,8},{8,0},{16,24},{24,16},{1,9},{9,1},{17,25},{25,17},{2,10},{10... | collective-permute-start | bytes 49160 | tf_op jit(solution)/shard_map/ppermute | solution.py:328
  59.3 1.8 %collective-permute-done.19.rec = f32[4,8,128]{2,1,0:T(8,128)S(1)} collective-permute-done((f32[4,8,128]{2,1,0:T(8,128)S(1)}, f32[4,8,128]{2,1,0:T(8,128)S(1)}, u32[]{:S(2)}, u32[]{:S(2)}) %collective-permute-start.19) | collective-permute-done | bytes 16416 | tf_op jit(solution)/shard_map/ppermute | solution.py:328
  61.0 1.5 %collective-permute-start.20 = (f32[4,8,128]{2,1,0:T(8,128)S(1)}, f32[4,8,128]{2,1,0:T(8,128)S(1)}, u32[]{:S(2)}, u32[]{:S(2)}) collective-permute-start(f32[4,8,128]{2,1,0:T(8,128)S(1)} %merge.10.mine), channel_id=1, source_target_pairs={{0,16},{8,24},{16,0},{24,8},{1,17},{9,25},{17,1},{25,9},{2,18},{10... | collective-permute-start | bytes 49160 | tf_op jit(solution)/shard_map/ppermute | solution.py:328
  62.5 2.2 %collective-permute-done.20.rec = f32[4,8,128]{2,1,0:T(8,128)S(1)} collective-permute-done((f32[4,8,128]{2,1,0:T(8,128)S(1)}, f32[4,8,128]{2,1,0:T(8,128)S(1)}, u32[]{:S(2)}, u32[]{:S(2)}) %collective-permute-start.20) | collective-permute-done | bytes 16416 | tf_op jit(solution)/shard_map/ppermute | solution.py:328
  64.8 3.8 %margin.1 = (f32[4,12,128]{2,1,0:T(8,128)S(1)}, f32[4,8,128]{2,1,0:T(8,128)S(1)}) custom-call(f32[1024,1536]{1,0:T(8,128)S(1)} %get-tuple-element.19.sim, f32[4,12,128]{2,1,0:T(8,128)S(1)} %merge.9.fwd_mine, f32[4,12,128]{2,1,0:T(8,128)S(1)} %collective-permute-done.18.fwd_other, f32[4,8,128]{2,1,0:T(8,128)S(1)} %merge.11.bwd_all), custom_call_target="tpu_custom_call" | custom-call | flops 47185920 | bytes 6291456 | tf_op jit(solution)/shard_map/margin/pallas_call | solution.py:394
  68.6 3.9 %collective-permute-done.21.rec = f32[4,12,128]{2,1,0:T(8,128)S(1)} collective-permute-done((f32[4,12,128]{2,1,0:T(8,128)S(1)}, f32[4,12,128]{2,1,0:T(8,128)S(1)}, u32[]{:S(2)}, u32[]{:S(2)}) %collective-permute-start.21) | collective-permute-done | bytes 24608 | tf_op jit(solution)/shard_map/ppermute | solution.py:325
  72.5 1.5 %collective-permute-start.22 = (f32[4,12,128]{2,1,0:T(8,128)S(1)}, f32[4,12,128]{2,1,0:T(8,128)S(1)}, u32[]{:S(2)}, u32[]{:S(2)}) collective-permute-start(f32[4,12,128]{2,1,0:T(8,128)S(1)} %merge.12.mine), channel_id=1, source_target_pairs={{0,4},{1,5},{2,6},{3,7},{4,0},{5,1},{6,2},{7,3},{8,12},{9,13},{10,... | collective-permute-start | bytes 73736 | tf_op jit(solution)/shard_map/ppermute | solution.py:325
  74.1 1.5 %collective-permute-start.24 = (f32[4,8,128]{2,1,0:T(8,128)S(1)}, f32[4,8,128]{2,1,0:T(8,128)S(1)}, u32[]{:S(2)}, u32[]{:S(2)}) collective-permute-start(f32[4,8,128]{2,1,0:T(8,128)S(1)} %get-tuple-element.23.mine), channel_id=1, source_target_pairs={{0,8},{8,0},{16,24},{24,16},{1,9},{9,1},{17,25},{25,17},{2,10},{10... | collective-permute-start | bytes 49160 | tf_op jit(solution)/shard_map/ppermute | solution.py:328
  75.6 1.9 %collective-permute-done.22.rec = f32[4,12,128]{2,1,0:T(8,128)S(1)} collective-permute-done((f32[4,12,128]{2,1,0:T(8,128)S(1)}, f32[4,12,128]{2,1,0:T(8,128)S(1)}, u32[]{:S(2)}, u32[]{:S(2)}) %collective-permute-start.22) | collective-permute-done | bytes 24608 | tf_op jit(solution)/shard_map/ppermute | solution.py:325
  77.8 1.5 %collective-permute-start.25 = (f32[4,8,128]{2,1,0:T(8,128)S(1)}, f32[4,8,128]{2,1,0:T(8,128)S(1)}, u32[]{:S(2)}, u32[]{:S(2)}) collective-permute-start(f32[4,8,128]{2,1,0:T(8,128)S(1)} %merge.14.mine), channel_id=1, source_target_pairs={{0,16},{8,24},{16,0},{24,8},{1,17},{9,25},{17,1},{25,9},{2,18},{10... | collective-permute-start | bytes 49160 | tf_op jit(solution)/shard_map/ppermute | solution.py:328
  79.3 2.2 %collective-permute-done.25.rec = f32[4,8,128]{2,1,0:T(8,128)S(1)} collective-permute-done((f32[4,8,128]{2,1,0:T(8,128)S(1)}, f32[4,8,128]{2,1,0:T(8,128)S(1)}, u32[]{:S(2)}, u32[]{:S(2)}) %collective-permute-start.25) | collective-permute-done | bytes 16416 | tf_op jit(solution)/shard_map/ppermute | solution.py:328
  81.5 0.6 final.1
  (33 shorter events, 2.1 us)
Async XLA Ops:
  0.6 12.7 %collective-permute-start.2 = (bf16[128,1536]{1,0:T(8,128)(2,1)}, bf16[128,1536]{1,0:T(8,128)(2,1)S(1)}, u32[]{:S(2)}, u32[]{:S(2)}) collective-permute-start(bf16[128,1536]{1,0:T(8,128)(2,1)} %refs_1_.1), channel_id=1, source_target_pairs={{0,1},{1,0},{2,3},{3,2},{4,5},{5,4},{6,7},{7,6},{8,9},{9,8},{10,11... | collective-permute-start | bytes 1179656 | tf_op jit(solution)/shard_map/ppermute | solution.py:296
  1.2 13.4 %collective-permute-start = (bf16[128,1536]{1,0:T(8,128)(2,1)}, bf16[128,1536]{1,0:T(8,128)(2,1)S(1)}, u32[]{:S(2)}, u32[]{:S(2)}) collective-permute-start(bf16[128,1536]{1,0:T(8,128)(2,1)} %refs_1_.1), channel_id=1, source_target_pairs={{0,4},{2,6},{5,1},{7,3},{8,12},{10,14},{13,9},{15,11},{16,20},{18,... | collective-permute-start | bytes 1179656 | tf_op jit(solution)/shard_map/ppermute | solution.py:307
  6.7 13.3 %collective-permute-start.7 = (bf16[256,1024]{1,0:T(8,128)(2,1)}, bf16[256,1024]{1,0:T(8,128)(2,1)S(1)}, u32[]{:S(2)}, u32[]{:S(2)}) collective-permute-start(bf16[256,1024]{1,0:T(8,128)(2,1)} %refs_0_.1), channel_id=1, source_target_pairs={{0,8},{1,17},{2,10},{3,19},{4,12},{5,21},{6,14},{7,23},{8,0},{9,25... | collective-permute-start | bytes 1572872 | tf_op jit(solution)/shard_map/ppermute | solution.py:314
  8.3 12.3 %collective-permute-start.8 = (bf16[256,1024]{1,0:T(8,128)(2,1)}, bf16[256,1024]{1,0:T(8,128)(2,1)S(1)}, u32[]{:S(2)}, u32[]{:S(2)}) collective-permute-start(bf16[256,1024]{1,0:T(8,128)(2,1)} %refs_0_.1), channel_id=1, source_target_pairs={{0,16},{1,9},{2,18},{3,11},{4,20},{5,13},{6,22},{7,15},{8,24},{9,1... | collective-permute-start | bytes 1572872 | tf_op jit(solution)/shard_map/ppermute | solution.py:314
  9.8 10.1 %collective-permute-start.10 = (bf16[128,1536]{1,0:T(8,128)(2,1)}, bf16[128,1536]{1,0:T(8,128)(2,1)S(1)}, u32[]{:S(2)}, u32[]{:S(2)}) collective-permute-start(bf16[128,1536]{1,0:T(8,128)(2,1)} %refs_1_.1), channel_id=1, source_target_pairs={{0,2},{2,4},{3,1},{4,6},{5,3},{7,5},{8,10},{10,12},{11,9},{12,14},... | collective-permute-start | bytes 1179656 | tf_op jit(solution)/shard_map/ppermute | solution.py:307
  13.3 9.7 %collective-permute-start.3 = (bf16[128,1536]{1,0:T(8,128)(2,1)S(1)}, bf16[128,1536]{1,0:T(8,128)(2,1)S(1)}, u32[]{:S(2)}, u32[]{:S(2)}) collective-permute-start(bf16[128,1536]{1,0:T(8,128)(2,1)S(1)} %collective-permute-done.2.refs_2_), channel_id=1, source_target_pairs={{0,4},{2,6},{5,1},{7,3},{8,12},{10,14},{13,9},{15,11},{16,20},{18,... | collective-permute-start | bytes 1179656 | tf_op jit(solution)/shard_map/ppermute | solution.py:307
  14.6 12.6 %collective-permute-start.11 = (bf16[128,1536]{1,0:T(8,128)(2,1)S(1)}, bf16[128,1536]{1,0:T(8,128)(2,1)S(1)}, u32[]{:S(2)}, u32[]{:S(2)}) collective-permute-start(bf16[128,1536]{1,0:T(8,128)(2,1)S(1)} %collective-permute-done.2.refs_2_), channel_id=1, source_target_pairs={{0,2},{2,4},{3,1},{4,6},{5,3},{7,5},{8,10},{10,12},{11,9},{12,14},... | collective-permute-start | bytes 1179656 | tf_op jit(solution)/shard_map/ppermute | solution.py:307
  19.9 7.8 %collective-permute-start.14 = (bf16[128,1536]{1,0:T(8,128)(2,1)S(1)}, bf16[128,1536]{1,0:T(8,128)(2,1)S(1)}, u32[]{:S(2)}, u32[]{:S(2)}) collective-permute-start(bf16[128,1536]{1,0:T(8,128)(2,1)S(1)} %collective-permute-done.refs_7_), channel_id=1, source_target_pairs={{0,1},{1,0},{2,3},{3,2},{4,5},{5,4},{6,7},{7,6},{8,9},{9,8},{10,11... | collective-permute-start | bytes 1179656 | tf_op jit(solution)/shard_map/ppermute | solution.py:296
  20.0 11.9 %collective-permute-start.12 = (bf16[128,1536]{1,0:T(8,128)(2,1)S(1)}, bf16[128,1536]{1,0:T(8,128)(2,1)S(1)}, u32[]{:S(2)}, u32[]{:S(2)}) collective-permute-start(bf16[128,1536]{1,0:T(8,128)(2,1)S(1)} %collective-permute-done.10.refs_3_), channel_id=1, source_target_pairs={{0,1},{1,0},{2,3},{3,2},{4,5},{5,4},{6,7},{7,6},{8,9},{9,8},{10,11... | collective-permute-start | bytes 1179656 | tf_op jit(solution)/shard_map/ppermute | solution.py:296
  20.5 11.4 %collective-permute-start.1 = (bf16[128,1536]{1,0:T(8,128)(2,1)S(1)}, bf16[128,1536]{1,0:T(8,128)(2,1)S(1)}, u32[]{:S(2)}, u32[]{:S(2)}) collective-permute-start(bf16[128,1536]{1,0:T(8,128)(2,1)S(1)} %collective-permute-done.refs_7_), channel_id=1, source_target_pairs={{3,1},{4,6},{11,9},{12,14},{19,17},{20,22},{27,25},{28,30}} | collective-permute-start | bytes 1179656 | tf_op jit(solution)/shard_map/ppermute | solution.py:307
  23.0 10.4 %collective-permute-start.4 = (bf16[128,1536]{1,0:T(8,128)(2,1)S(1)}, bf16[128,1536]{1,0:T(8,128)(2,1)S(1)}, u32[]{:S(2)}, u32[]{:S(2)}) collective-permute-start(bf16[128,1536]{1,0:T(8,128)(2,1)S(1)} %collective-permute-done.3.refs_8_), channel_id=1, source_target_pairs={{3,1},{4,6},{11,9},{12,14},{19,17},{20,22},{27,25},{28,30}} | collective-permute-start | bytes 1179656 | tf_op jit(solution)/shard_map/ppermute | solution.py:307
  27.2 11.3 %collective-permute-start.9 = (bf16[256,1024]{1,0:T(8,128)(2,1)S(1)}, bf16[256,1024]{1,0:T(8,128)(2,1)S(1)}, u32[]{:S(2)}, u32[]{:S(2)}) collective-permute-start(bf16[256,1024]{1,0:T(8,128)(2,1)S(1)} %collective-permute-done.7.refs_0_), channel_id=1, source_target_pairs={{0,16},{1,9},{2,18},{3,11},{4,20},{5,13},{6,22},{7,15},{8,24},{9,1... | collective-permute-start | bytes 1572872 | tf_op jit(solution)/shard_map/ppermute | solution.py:314
  27.7 10.8 %collective-permute-start.15 = (bf16[128,1536]{1,0:T(8,128)(2,1)S(1)}, bf16[128,1536]{1,0:T(8,128)(2,1)S(1)}, u32[]{:S(2)}, u32[]{:S(2)}) collective-permute-start(bf16[128,1536]{1,0:T(8,128)(2,1)S(1)} %collective-permute-done.3.refs_8_), channel_id=1, source_target_pairs={{0,1},{1,0},{2,3},{3,2},{4,5},{5,4},{6,7},{7,6},{8,9},{9,8},{10,11... | collective-permute-start | bytes 1179656 | tf_op jit(solution)/shard_map/ppermute | solution.py:296
  31.9 6.7 %collective-permute-start.13 = (bf16[128,1536]{1,0:T(8,128)(2,1)S(1)}, bf16[128,1536]{1,0:T(8,128)(2,1)S(1)}, u32[]{:S(2)}, u32[]{:S(2)}) collective-permute-start(bf16[128,1536]{1,0:T(8,128)(2,1)S(1)} %collective-permute-done.11.refs_4_), channel_id=1, source_target_pairs={{0,1},{1,0},{2,3},{3,2},{4,5},{5,4},{6,7},{7,6},{8,9},{9,8},{10,11... | collective-permute-start | bytes 1179656 | tf_op jit(solution)/shard_map/ppermute | solution.py:296
  32.0 7.8 %collective-permute-start.5 = (bf16[128,1536]{1,0:T(8,128)(2,1)S(1)}, bf16[128,1536]{1,0:T(8,128)(2,1)S(1)}, u32[]{:S(2)}, u32[]{:S(2)}) collective-permute-start(bf16[128,1536]{1,0:T(8,128)(2,1)S(1)} %collective-permute-done.1.refs_0_), channel_id=1, source_target_pairs={{0,1},{1,0},{2,3},{3,2},{4,5},{5,4},{6,7},{7,6},{8,9},{9,8},{10,11... | collective-permute-start | bytes 1179656 | tf_op jit(solution)/shard_map/ppermute | solution.py:296
  33.4 6.4 %collective-permute-start.6 = (bf16[128,1536]{1,0:T(8,128)(2,1)S(1)}, bf16[128,1536]{1,0:T(8,128)(2,1)S(1)}, u32[]{:S(2)}, u32[]{:S(2)}) collective-permute-start(bf16[128,1536]{1,0:T(8,128)(2,1)S(1)} %collective-permute-done.4.refs_1_), channel_id=1, source_target_pairs={{0,1},{1,0},{2,3},{3,2},{4,5},{5,4},{6,7},{7,6},{8,9},{9,8},{10,11... | collective-permute-start | bytes 1179656 | tf_op jit(solution)/shard_map/ppermute | solution.py:296
  45.9 7.3 %collective-permute-start.16 = (f32[4,12,128]{2,1,0:T(8,128)S(1)}, f32[4,12,128]{2,1,0:T(8,128)S(1)}, u32[]{:S(2)}, u32[]{:S(2)}) collective-permute-start(f32[4,12,128]{2,1,0:T(8,128)S(1)} %get-tuple-element.20.mine), channel_id=1, source_target_pairs={{0,2},{1,3},{2,0},{3,1},{4,6},{5,7},{6,4},{7,5},{8,10},{9,11},{10,... | collective-permute-start | bytes 73736 | tf_op jit(solution)/shard_map/ppermute | solution.py:325
  53.2 5.9 %collective-permute-start.17 = (f32[4,12,128]{2,1,0:T(8,128)S(1)}, f32[4,12,128]{2,1,0:T(8,128)S(1)}, u32[]{:S(2)}, u32[]{:S(2)}) collective-permute-start(f32[4,12,128]{2,1,0:T(8,128)S(1)} %merge.8.mine), channel_id=1, source_target_pairs={{0,4},{1,5},{2,6},{3,7},{4,0},{5,1},{6,2},{7,3},{8,12},{9,13},{10,... | collective-permute-start | bytes 73736 | tf_op jit(solution)/shard_map/ppermute | solution.py:325
  57.3 3.7 %collective-permute-start.19 = (f32[4,8,128]{2,1,0:T(8,128)S(1)}, f32[4,8,128]{2,1,0:T(8,128)S(1)}, u32[]{:S(2)}, u32[]{:S(2)}) collective-permute-start(f32[4,8,128]{2,1,0:T(8,128)S(1)} %get-tuple-element.21.mine), channel_id=1, source_target_pairs={{0,8},{8,0},{16,24},{24,16},{1,9},{9,1},{17,25},{25,17},{2,10},{10... | collective-permute-start | bytes 49160 | tf_op jit(solution)/shard_map/ppermute | solution.py:328
  59.2 5.6 %collective-permute-start.18 = (f32[4,12,128]{2,1,0:T(8,128)S(1)}, f32[4,12,128]{2,1,0:T(8,128)S(1)}, u32[]{:S(2)}, u32[]{:S(2)}) collective-permute-start(f32[4,12,128]{2,1,0:T(8,128)S(1)} %merge.9.fwd_mine), channel_id=1, source_target_pairs={{0,1},{1,0},{2,3},{3,2},{4,5},{5,4},{6,7},{7,6},{8,9},{9,8},{10,11... | collective-permute-start | bytes 73736 | tf_op jit(solution)/shard_map/ppermute | solution.py:296
  61.0 3.7 %collective-permute-start.20 = (f32[4,8,128]{2,1,0:T(8,128)S(1)}, f32[4,8,128]{2,1,0:T(8,128)S(1)}, u32[]{:S(2)}, u32[]{:S(2)}) collective-permute-start(f32[4,8,128]{2,1,0:T(8,128)S(1)} %merge.10.mine), channel_id=1, source_target_pairs={{0,16},{8,24},{16,0},{24,8},{1,17},{9,25},{17,1},{25,9},{2,18},{10... | collective-permute-start | bytes 49160 | tf_op jit(solution)/shard_map/ppermute | solution.py:328
  68.5 4.0 %collective-permute-start.21 = (f32[4,12,128]{2,1,0:T(8,128)S(1)}, f32[4,12,128]{2,1,0:T(8,128)S(1)}, u32[]{:S(2)}, u32[]{:S(2)}) collective-permute-start(f32[4,12,128]{2,1,0:T(8,128)S(1)} %get-tuple-element.22.mine), channel_id=1, source_target_pairs={{0,2},{1,3},{2,0},{3,1},{4,6},{5,7},{6,4},{7,5},{8,10},{9,11},{10,... | collective-permute-start | bytes 73736 | tf_op jit(solution)/shard_map/ppermute | solution.py:325
  72.5 4.9 %collective-permute-start.22 = (f32[4,12,128]{2,1,0:T(8,128)S(1)}, f32[4,12,128]{2,1,0:T(8,128)S(1)}, u32[]{:S(2)}, u32[]{:S(2)}) collective-permute-start(f32[4,12,128]{2,1,0:T(8,128)S(1)} %merge.12.mine), channel_id=1, source_target_pairs={{0,4},{1,5},{2,6},{3,7},{4,0},{5,1},{6,2},{7,3},{8,12},{9,13},{10,... | collective-permute-start | bytes 73736 | tf_op jit(solution)/shard_map/ppermute | solution.py:325
  74.1 3.7 %collective-permute-start.24 = (f32[4,8,128]{2,1,0:T(8,128)S(1)}, f32[4,8,128]{2,1,0:T(8,128)S(1)}, u32[]{:S(2)}, u32[]{:S(2)}) collective-permute-start(f32[4,8,128]{2,1,0:T(8,128)S(1)} %get-tuple-element.23.mine), channel_id=1, source_target_pairs={{0,8},{8,0},{16,24},{24,16},{1,9},{9,1},{17,25},{25,17},{2,10},{10... | collective-permute-start | bytes 49160 | tf_op jit(solution)/shard_map/ppermute | solution.py:328
  77.4 4.1 %collective-permute-start.23 = (f32[4,12,128]{2,1,0:T(8,128)S(1)}, f32[4,12,128]{2,1,0:T(8,128)S(1)}, u32[]{:S(2)}, u32[]{:S(2)}) collective-permute-start(f32[4,12,128]{2,1,0:T(8,128)S(1)} %merge.13.fwd_mine), channel_id=1, source_target_pairs={{0,1},{1,0},{2,3},{3,2},{4,5},{5,4},{6,7},{7,6},{8,9},{9,8},{10,11... | collective-permute-start | bytes 73736 | tf_op jit(solution)/shard_map/ppermute | solution.py:296
  77.8 3.7 %collective-permute-start.25 = (f32[4,8,128]{2,1,0:T(8,128)S(1)}, f32[4,8,128]{2,1,0:T(8,128)S(1)}, u32[]{:S(2)}, u32[]{:S(2)}) collective-permute-start(f32[4,8,128]{2,1,0:T(8,128)S(1)} %merge.14.mine), channel_id=1, source_target_pairs={{0,16},{8,24},{16,0},{24,8},{1,17},{9,25},{17,1},{25,9},{2,18},{10... | collective-permute-start | bytes 49160 | tf_op jit(solution)/shard_map/ppermute | solution.py:328

commit v3 on v0

--- a/solution.py
+++ b/solution.py
@@ -268,6 +268,10 @@
             backward[pl.ds(k, 1), pl.ds(c * LANES, LANES)] = bwd_all[k, pl.ds(c, 1), :]
 
 
+def in_hbm(x):
+    return pltpu.with_memory_space_constraint(x, pltpu.HBM)
+
+
 def f32(*shape):
     return jax.ShapeDtypeStruct(shape, jnp.float32)
 
@@ -350,6 +354,8 @@
 
         def prep(tgt, steps, extra, first):
             src = (own if first else []) + [x for k in steps for x in passed[k]]
+            if first:
+                tgt, src = [(in_hbm(tgt[0][0]), tgt[0][1])], [in_hbm(src[0]), src[1]]
             shapes = [jax.ShapeDtypeStruct((total, targets), tgt_codes.dtype),
                       jax.ShapeDtypeStruct((total, sources), src_codes.dtype)]
             sems = [pltpu.SemaphoreType.DMA((len(tgt),)), pltpu.SemaphoreType.DMA((max(len(src), 1),))]
@@ -366,8 +372,8 @@
                 compiler_params=params(2), cost_estimate=cost(0, 4 * total * targets))(*[x for x, _ in tgt], *src, *extra)
 
         steps = list(range(1, depth - 1))
-        tgt_block, src_block, column, lane = prep(held[:1], steps[:-1], (scale_s, scale_t), True)
-        tgt_block, src_block = prep(held[1:], steps[-1:], (tgt_block, src_block), False)
+        tgt_block, src_block, column, lane = prep(held[:1], [], (in_hbm(scale_s), in_hbm(scale_t)), True)
+        tgt_block, src_block = prep(held[1:], steps, (tgt_block, src_block), False)
         block = min(512, targets // 2)
         _, sim, fwd, bwd = pl.pallas_call(
             functools.partial(score_kernel, depth),

time: 78.7 us -> 75.6 us (0.961)
  waiting for transfers between devices: 21.1 us -> 27 us
  starting transfers between devices: 40.4 us -> 34.6 us
  local copies, waits for them, and re-layouts: 3.42 us -> 0 us
    ppermute x3, waiting for transfers between devices: 3.12 us -> 10.1 us  [along_src(): return lax.ppermute(x, both, pairs)]
    ppermute x9, starting transfers between devices: 11.1 us -> 4.4 us  [swap(): return lax.ppermute(x, 'tgt', partner)]
    unnamed x8 -> x0, local copies, waits for them, and re-layouts: 3.42 us -> none
    ppermute x4, waiting for transfers between devices: 8.04 us -> 6.85 us  [reduce_lists(): from_z = lax.ppermute(fwd, 'tgt', pairs)]
    ppermute x4, starting transfers between devices: 7.9 us -> 8.84 us  [reduce_lists(): from_z = lax.ppermute(fwd, 'tgt', pairs)]
  transfers between devices with their start and end apart: 26 -> 26, of which waited for: 11 -> 13; matrix products, arithmetic and copies ran while one was open for 0% -> 0% of each run, Pallas kernels for 2% -> 3%
where the time goes in v3:
time: 75.6 us; the launch traced here: 75.4 us
  starting transfers between devices  34.6 us (46%)
  waiting for transfers between devices  27 us (36%)
  Pallas kernels  12.9 us (17%)
  between operations  0.81 us (1%)
    ppermute x6, starting transfers between devices, along_z(): return lax.ppermute(x, 'tgt', pairs)  10.7 us
    ppermute x3, waiting for transfers between devices, along_src(): return lax.ppermute(x, both, pairs)  10.1 us
    ppermute x4, starting transfers between devices, reduce_lists(): from_z = lax.ppermute(fwd, 'tgt', pairs)  8.84 us
    ppermute x4, waiting for transfers between devices, reduce_lists(): from_z = lax.ppermute(fwd, 'tgt', pairs)  6.85 us
    ppermute x4, waiting for transfers between devices, reduce_lists(): from_src = lax.ppermute(bwd, 'src', pairs)  6.11 us
    pallas_call x1, Pallas kernels, compute(): pl.pallas_call(functools.partial(score_kernel, depth), out_shape=(jax.Sha...  6.07 us
    ppermute x4, starting transfers between devices, reduce_lists(): from_src = lax.ppermute(bwd, 'src', pairs)  6.03 us
    ppermute x3, starting transfers between devices, along_src(): return lax.ppermute(x, both, pairs)  4.66 us
  transfers between devices with their start and end apart: 26, of which 13 were waited for; matrix products, arithmetic and copies ran while one was open for 0% of the time, Pallas kernels for 3%

profile of v3, /device:TPU:0, one launch (start us, length us, event | category | flops | bytes accessed | tf_op | source)
XLA Modules:
  0.0 75.4 jit_solution(4548475516331573231)
XLA Ops:
  1.2 4.5 %collective-permute-start = (bf16[128,1536]{1,0:T(8,128)(2,1)}, bf16[128,1536]{1,0:T(8,128)(2,1)S(1)}, u32[]{:S(2)}, u32[]{:S(2)}) collective-permute-start(bf16[128,1536]{1,0:T(8,128)(2,1)} %refs_1_.1), channel_id=1, source_target_pairs={{0,2},{2,4},{3,1},{4,6},{5,3},{7,5},{8,10},{10,12},{11,9},{12,14},... | collective-permute-start | bytes 1179656 | tf_op jit(solution)/shard_map/ppermute | solution.py:306
  5.7 3.5 %collective-permute-start.4 = (bf16[128,1536]{1,0:T(8,128)(2,1)S(1)}, bf16[128,1536]{1,0:T(8,128)(2,1)S(1)}, u32[]{:S(2)}, u32[]{:S(2)}) collective-permute-start(bf16[128,1536]{1,0:T(8,128)(2,1)S(1)} %collective-permute-done.3.refs_2_), channel_id=1, source_target_pairs={{0,2},{2,4},{3,1},{4,6},{5,3},{7,5},{8,10},{10,12},{11,9},{12,14},... | collective-permute-start | bytes 1179656 | tf_op jit(solution)/shard_map/ppermute | solution.py:306
  9.2 1.6 %collective-permute-start.9 = (bf16[256,1024]{1,0:T(8,128)(2,1)}, bf16[256,1024]{1,0:T(8,128)(2,1)S(1)}, u32[]{:S(2)}, u32[]{:S(2)}) collective-permute-start(bf16[256,1024]{1,0:T(8,128)(2,1)} %refs_0_.1), channel_id=1, source_target_pairs={{0,8},{1,17},{2,10},{3,19},{4,12},{5,21},{6,14},{7,23},{8,0},{9,25... | collective-permute-start | bytes 1572872 | tf_op jit(solution)/shard_map/ppermute | solution.py:313
  11.3 0.7 collective-permute-start.1
  11.9 3.4 %collective-permute-done.4.refs_4_ = bf16[128,1536]{1,0:T(8,128)(2,1)S(1)} collective-permute-done((bf16[128,1536]{1,0:T(8,128)(2,1)S(1)}, bf16[128,1536]{1,0:T(8,128)(2,1)S(1)}, u32[]{:S(2)}, u32[]{:S(2)}) %collective-permute-start.4) | collective-permute-done | bytes 393248 | tf_op jit(solution)/shard_map/ppermute | solution.py:306
  15.4 0.7 collective-permute-start.5
  16.1 1.6 %collective-permute-start.10 = (bf16[256,1024]{1,0:T(8,128)(2,1)}, bf16[256,1024]{1,0:T(8,128)(2,1)S(1)}, u32[]{:S(2)}, u32[]{:S(2)}) collective-permute-start(bf16[256,1024]{1,0:T(8,128)(2,1)} %refs_0_.1), channel_id=1, source_target_pairs={{0,16},{1,9},{2,18},{3,11},{4,20},{5,13},{6,22},{7,15},{8,24},{9,1... | collective-permute-start | bytes 1572872 | tf_op jit(solution)/shard_map/ppermute | solution.py:313
  17.6 1.0 %collective-permute-done.9.refs_0_ = bf16[256,1024]{1,0:T(8,128)(2,1)S(1)} collective-permute-done((bf16[256,1024]{1,0:T(8,128)(2,1)}, bf16[256,1024]{1,0:T(8,128)(2,1)S(1)}, u32[]{:S(2)}, u32[]{:S(2)}) %collective-permute-start.9) | collective-permute-done | bytes 524320 | tf_op jit(solution)/shard_map/ppermute | solution.py:313
  18.7 1.5 %collective-permute-start.11 = (bf16[256,1024]{1,0:T(8,128)(2,1)S(1)}, bf16[256,1024]{1,0:T(8,128)(2,1)S(1)}, u32[]{:S(2)}, u32[]{:S(2)}) collective-permute-start(bf16[256,1024]{1,0:T(8,128)(2,1)S(1)} %collective-permute-done.9.refs_0_), channel_id=1, source_target_pairs={{0,16},{1,9},{2,18},{3,11},{4,20},{5,13},{6,22},{7,15},{8,24},{9,1... | collective-permute-start | bytes 1572872 | tf_op jit(solution)/shard_map/ppermute | solution.py:313
  20.2 0.7 collective-permute-start.2
  20.9 0.7 collective-permute-start.6
  21.6 3.9 %collective-permute-done.10.refs_1_ = bf16[256,1024]{1,0:T(8,128)(2,1)S(1)} collective-permute-done((bf16[256,1024]{1,0:T(8,128)(2,1)}, bf16[256,1024]{1,0:T(8,128)(2,1)S(1)}, u32[]{:S(2)}, u32[]{:S(2)}) %collective-permute-start.10) | collective-permute-done | bytes 524320 | tf_op jit(solution)/shard_map/ppermute | solution.py:313
  26.0 5.1 %collective-permute-done.11.refs_2_ = bf16[256,1024]{1,0:T(8,128)(2,1)S(1)} collective-permute-done((bf16[256,1024]{1,0:T(8,128)(2,1)S(1)}, bf16[256,1024]{1,0:T(8,128)(2,1)S(1)}, u32[]{:S(2)}, u32[]{:S(2)}) %collective-permute-start.11) | collective-permute-done | bytes 524320 | tf_op jit(solution)/shard_map/ppermute | solution.py:313
  31.6 2.7 %collective-permute-start.8 = (bf16[128,1536]{1,0:T(8,128)(2,1)S(1)}, bf16[128,1536]{1,0:T(8,128)(2,1)S(1)}, u32[]{:S(2)}, u32[]{:S(2)}) collective-permute-start(bf16[128,1536]{1,0:T(8,128)(2,1)S(1)} %collective-permute-done.6.refs_1_), channel_id=1, source_target_pairs={{0,1},{1,0},{2,3},{3,2},{4,5},{5,4},{6,7},{7,6},{8,9},{9,8},{10,11... | collective-permute-start | bytes 1179656 | tf_op jit(solution)/shard_map/ppermute | solution.py:296
  34.3 1.2 %shard_map.59 = (bf16[1024,1024]{1,0:T(8,128)(2,1)S(1)}, bf16[1024,1536]{1,0:T(8,128)(2,1)S(1)}, f32[1024,128]{1,0:T(8,128)S(1)}, f32[8,1536]{1,0:T(8,128)S(1)}) custom-call(bf16[256,1024]{1,0:T(8,128)(2,1)} %refs_0_.1, bf16[128,1536]{1,0:T(8,128)(2,1)} %refs_1_.1, bf16[128,1536]{1,0:T(8,128)(2,1)S(1)} %collective-permute-done.3.refs_2_, f32[12,128]{1,0:T(8,128)} %bitcast.2, ...), custom_call_target="tpu_custom_call" | custom-call | bytes 4194304 | tf_op jit(solution)/shard_map/pallas_call | solution.py:367
  35.6 1.2 %shard_map.60 = (bf16[1024,1024]{1,0:T(8,128)(2,1)S(1)}, bf16[1024,1536]{1,0:T(8,128)(2,1)S(1)}) custom-call(bf16[256,1024]{1,0:T(8,128)(2,1)S(1)} %collective-permute-done.9.refs_0_, bf16[256,1024]{1,0:T(8,128)(2,1)S(1)} %collective-permute-done.10.refs_1_, ...), custom_call_target="tpu_custom_call", output_to_operand_aliasing={{0}: (11, {}), {1}: (12, {})} | custom-call | bytes 4194304 | tf_op jit(solution)/shard_map/pallas_call | solution.py:367
  36.8 6.1 %score.1 = (bf16[1024,1536]{1,0:T(8,128)(2,1)S(1)}, f32[1024,1536]{1,0:T(8,128)S(1)}, f32[4,12,128]{2,1,0:T(8,128)S(1)}, f32[4,8,128]{2,1,0:T(8,128)S(1)}) custom-call(bf16[128,1536]{1,0:T(8,128)(2,1)S(1)} %collective-permute-done.2.refs_0_, bf16[128,1536]{1,0:T(8,128)(2,1)S(1)} %collective-permute-done.6.refs_1_, ...), custom_call_target="tpu_custom_call", output_to_operand_aliasing={{0}: (5, {})} | custom-call | flops 3221225472 | bytes 6291456 | tf_op jit(solution)/shard_map/score/pallas_call | solution.py:378
  42.9 2.8 %collective-permute-start.16 = (f32[4,12,128]{2,1,0:T(8,128)S(1)}, f32[4,12,128]{2,1,0:T(8,128)S(1)}, u32[]{:S(2)}, u32[]{:S(2)}) collective-permute-start(f32[4,12,128]{2,1,0:T(8,128)S(1)} %get-tuple-element.20.mine), channel_id=1, source_target_pairs={{0,2},{1,3},{2,0},{3,1},{4,6},{5,7},{6,4},{7,5},{8,10},{9,11},{10,... | collective-permute-start | bytes 73736 | tf_op jit(solution)/shard_map/ppermute | solution.py:324
  45.7 2.0 %collective-permute-done.16.rec = f32[4,12,128]{2,1,0:T(8,128)S(1)} collective-permute-done((f32[4,12,128]{2,1,0:T(8,128)S(1)}, f32[4,12,128]{2,1,0:T(8,128)S(1)}, u32[]{:S(2)}, u32[]{:S(2)}) %collective-permute-start.16) | collective-permute-done | bytes 24608 | tf_op jit(solution)/shard_map/ppermute | solution.py:324
  47.7 3.0 %collective-permute-start.17 = (f32[4,12,128]{2,1,0:T(8,128)S(1)}, f32[4,12,128]{2,1,0:T(8,128)S(1)}, u32[]{:S(2)}, u32[]{:S(2)}) collective-permute-start(f32[4,12,128]{2,1,0:T(8,128)S(1)} %merge.8.mine), channel_id=1, source_target_pairs={{0,4},{1,5},{2,6},{3,7},{4,0},{5,1},{6,2},{7,3},{8,12},{9,13},{10,... | collective-permute-start | bytes 73736 | tf_op jit(solution)/shard_map/ppermute | solution.py:324
  50.6 1.5 %collective-permute-start.19 = (f32[4,8,128]{2,1,0:T(8,128)S(1)}, f32[4,8,128]{2,1,0:T(8,128)S(1)}, u32[]{:S(2)}, u32[]{:S(2)}) collective-permute-start(f32[4,8,128]{2,1,0:T(8,128)S(1)} %get-tuple-element.21.mine), channel_id=1, source_target_pairs={{0,8},{8,0},{16,24},{24,16},{1,9},{9,1},{17,25},{25,17},{2,10},{10... | collective-permute-start | bytes 49160 | tf_op jit(solution)/shard_map/ppermute | solution.py:327
  52.8 1.6 %collective-permute-done.19.rec = f32[4,8,128]{2,1,0:T(8,128)S(1)} collective-permute-done((f32[4,8,128]{2,1,0:T(8,128)S(1)}, f32[4,8,128]{2,1,0:T(8,128)S(1)}, u32[]{:S(2)}, u32[]{:S(2)}) %collective-permute-start.19) | collective-permute-done | bytes 16416 | tf_op jit(solution)/shard_map/ppermute | solution.py:327
  54.4 1.5 %collective-permute-start.20 = (f32[4,8,128]{2,1,0:T(8,128)S(1)}, f32[4,8,128]{2,1,0:T(8,128)S(1)}, u32[]{:S(2)}, u32[]{:S(2)}) collective-permute-start(f32[4,8,128]{2,1,0:T(8,128)S(1)} %merge.10.mine), channel_id=1, source_target_pairs={{0,16},{8,24},{16,0},{24,8},{1,17},{9,25},{17,1},{25,9},{2,18},{10... | collective-permute-start | bytes 49160 | tf_op jit(solution)/shard_map/ppermute | solution.py:327
  55.9 2.2 %collective-permute-done.20.rec = f32[4,8,128]{2,1,0:T(8,128)S(1)} collective-permute-done((f32[4,8,128]{2,1,0:T(8,128)S(1)}, f32[4,8,128]{2,1,0:T(8,128)S(1)}, u32[]{:S(2)}, u32[]{:S(2)}) %collective-permute-start.20) | collective-permute-done | bytes 16416 | tf_op jit(solution)/shard_map/ppermute | solution.py:327
  58.1 3.8 %margin.1 = (f32[4,12,128]{2,1,0:T(8,128)S(1)}, f32[4,8,128]{2,1,0:T(8,128)S(1)}) custom-call(f32[1024,1536]{1,0:T(8,128)S(1)} %get-tuple-element.19.sim, f32[4,12,128]{2,1,0:T(8,128)S(1)} %merge.9.fwd_mine, f32[4,12,128]{2,1,0:T(8,128)S(1)} %collective-permute-done.18.fwd_other, f32[4,8,128]{2,1,0:T(8,128)S(1)} %merge.11.bwd_all), custom_call_target="tpu_custom_call" | custom-call | flops 47185920 | bytes 6291456 | tf_op jit(solution)/shard_map/margin/pallas_call | solution.py:393
  61.9 1.8 %collective-permute-start.21 = (f32[4,12,128]{2,1,0:T(8,128)S(1)}, f32[4,12,128]{2,1,0:T(8,128)S(1)}, u32[]{:S(2)}, u32[]{:S(2)}) collective-permute-start(f32[4,12,128]{2,1,0:T(8,128)S(1)} %get-tuple-element.22.mine), channel_id=1, source_target_pairs={{0,2},{1,3},{2,0},{3,1},{4,6},{5,7},{6,4},{7,5},{8,10},{9,11},{10,... | collective-permute-start | bytes 73736 | tf_op jit(solution)/shard_map/ppermute | solution.py:324
  63.7 2.2 %collective-permute-done.21.rec = f32[4,12,128]{2,1,0:T(8,128)S(1)} collective-permute-done((f32[4,12,128]{2,1,0:T(8,128)S(1)}, f32[4,12,128]{2,1,0:T(8,128)S(1)}, u32[]{:S(2)}, u32[]{:S(2)}) %collective-permute-start.21) | collective-permute-done | bytes 24608 | tf_op jit(solution)/shard_map/ppermute | solution.py:324
  65.9 1.3 %collective-permute-start.22 = (f32[4,12,128]{2,1,0:T(8,128)S(1)}, f32[4,12,128]{2,1,0:T(8,128)S(1)}, u32[]{:S(2)}, u32[]{:S(2)}) collective-permute-start(f32[4,12,128]{2,1,0:T(8,128)S(1)} %merge.12.mine), channel_id=1, source_target_pairs={{0,4},{1,5},{2,6},{3,7},{4,0},{5,1},{6,2},{7,3},{8,12},{9,13},{10,... | collective-permute-start | bytes 73736 | tf_op jit(solution)/shard_map/ppermute | solution.py:324
  67.2 1.5 %collective-permute-start.24 = (f32[4,8,128]{2,1,0:T(8,128)S(1)}, f32[4,8,128]{2,1,0:T(8,128)S(1)}, u32[]{:S(2)}, u32[]{:S(2)}) collective-permute-start(f32[4,8,128]{2,1,0:T(8,128)S(1)} %get-tuple-element.23.mine), channel_id=1, source_target_pairs={{0,8},{8,0},{16,24},{24,16},{1,9},{9,1},{17,25},{25,17},{2,10},{10... | collective-permute-start | bytes 49160 | tf_op jit(solution)/shard_map/ppermute | solution.py:327
  68.7 2.1 %collective-permute-done.22.rec = f32[4,12,128]{2,1,0:T(8,128)S(1)} collective-permute-done((f32[4,12,128]{2,1,0:T(8,128)S(1)}, f32[4,12,128]{2,1,0:T(8,128)S(1)}, u32[]{:S(2)}, u32[]{:S(2)}) %collective-permute-start.22) | collective-permute-done | bytes 24608 | tf_op jit(solution)/shard_map/ppermute | solution.py:324
  71.0 1.5 %collective-permute-start.25 = (f32[4,8,128]{2,1,0:T(8,128)S(1)}, f32[4,8,128]{2,1,0:T(8,128)S(1)}, u32[]{:S(2)}, u32[]{:S(2)}) collective-permute-start(f32[4,8,128]{2,1,0:T(8,128)S(1)} %merge.14.mine), channel_id=1, source_target_pairs={{0,16},{8,24},{16,0},{24,8},{1,17},{9,25},{17,1},{25,9},{2,18},{10... | collective-permute-start | bytes 49160 | tf_op jit(solution)/shard_map/ppermute | solution.py:327
  72.5 2.2 %collective-permute-done.25.rec = f32[4,8,128]{2,1,0:T(8,128)S(1)} collective-permute-done((f32[4,8,128]{2,1,0:T(8,128)S(1)}, f32[4,8,128]{2,1,0:T(8,128)S(1)}, u32[]{:S(2)}, u32[]{:S(2)}) %collective-permute-start.25) | collective-permute-done | bytes 16416 | tf_op jit(solution)/shard_map/ppermute | solution.py:327
  (33 shorter events, 3.6 us)
Async XLA Ops:
  0.6 5.1 %collective-permute-start.3 = (bf16[128,1536]{1,0:T(8,128)(2,1)}, bf16[128,1536]{1,0:T(8,128)(2,1)S(1)}, u32[]{:S(2)}, u32[]{:S(2)}) collective-permute-start(bf16[128,1536]{1,0:T(8,128)(2,1)} %refs_1_.1), channel_id=1, source_target_pairs={{0,1},{1,0},{2,3},{3,2},{4,5},{5,4},{6,7},{7,6},{8,9},{9,8},{10,11... | collective-permute-start | bytes 1179656 | tf_op jit(solution)/shard_map/ppermute | solution.py:296
  1.2 10.1 %collective-permute-start = (bf16[128,1536]{1,0:T(8,128)(2,1)}, bf16[128,1536]{1,0:T(8,128)(2,1)S(1)}, u32[]{:S(2)}, u32[]{:S(2)}) collective-permute-start(bf16[128,1536]{1,0:T(8,128)(2,1)} %refs_1_.1), channel_id=1, source_target_pairs={{0,2},{2,4},{3,1},{4,6},{5,3},{7,5},{8,10},{10,12},{11,9},{12,14},... | collective-permute-start | bytes 1179656 | tf_op jit(solution)/shard_map/ppermute | solution.py:306
  5.7 9.7 %collective-permute-start.4 = (bf16[128,1536]{1,0:T(8,128)(2,1)S(1)}, bf16[128,1536]{1,0:T(8,128)(2,1)S(1)}, u32[]{:S(2)}, u32[]{:S(2)}) collective-permute-start(bf16[128,1536]{1,0:T(8,128)(2,1)S(1)} %collective-permute-done.3.refs_2_), channel_id=1, source_target_pairs={{0,2},{2,4},{3,1},{4,6},{5,3},{7,5},{8,10},{10,12},{11,9},{12,14},... | collective-permute-start | bytes 1179656 | tf_op jit(solution)/shard_map/ppermute | solution.py:306
  9.2 9.5 %collective-permute-start.9 = (bf16[256,1024]{1,0:T(8,128)(2,1)}, bf16[256,1024]{1,0:T(8,128)(2,1)S(1)}, u32[]{:S(2)}, u32[]{:S(2)}) collective-permute-start(bf16[256,1024]{1,0:T(8,128)(2,1)} %refs_0_.1), channel_id=1, source_target_pairs={{0,8},{1,17},{2,10},{3,19},{4,12},{5,21},{6,14},{7,23},{8,0},{9,25... | collective-permute-start | bytes 1572872 | tf_op jit(solution)/shard_map/ppermute | solution.py:313
  11.3 8.9 %collective-permute-start.1 = (bf16[128,1536]{1,0:T(8,128)(2,1)S(1)}, bf16[128,1536]{1,0:T(8,128)(2,1)S(1)}, u32[]{:S(2)}, u32[]{:S(2)}) collective-permute-start(bf16[128,1536]{1,0:T(8,128)(2,1)S(1)} %collective-permute-done.refs_3_), channel_id=1, source_target_pairs={{2,4},{3,1},{4,6},{5,3},{10,12},{11,9},{12,14},{13,11},{18,20},{19... | collective-permute-start | bytes 1179656 | tf_op jit(solution)/shard_map/ppermute | solution.py:306
  15.4 5.5 %collective-permute-start.5 = (bf16[128,1536]{1,0:T(8,128)(2,1)S(1)}, bf16[128,1536]{1,0:T(8,128)(2,1)S(1)}, u32[]{:S(2)}, u32[]{:S(2)}) collective-permute-start(bf16[128,1536]{1,0:T(8,128)(2,1)S(1)} %collective-permute-done.4.refs_4_), channel_id=1, source_target_pairs={{2,4},{3,1},{4,6},{5,3},{10,12},{11,9},{12,14},{13,11},{18,20},{19... | collective-permute-start | bytes 1179656 | tf_op jit(solution)/shard_map/ppermute | solution.py:306
  16.1 9.5 %collective-permute-start.10 = (bf16[256,1024]{1,0:T(8,128)(2,1)}, bf16[256,1024]{1,0:T(8,128)(2,1)S(1)}, u32[]{:S(2)}, u32[]{:S(2)}) collective-permute-start(bf16[256,1024]{1,0:T(8,128)(2,1)} %refs_0_.1), channel_id=1, source_target_pairs={{0,16},{1,9},{2,18},{3,11},{4,20},{5,13},{6,22},{7,15},{8,24},{9,1... | collective-permute-start | bytes 1572872 | tf_op jit(solution)/shard_map/ppermute | solution.py:313
  18.7 12.5 %collective-permute-start.11 = (bf16[256,1024]{1,0:T(8,128)(2,1)S(1)}, bf16[256,1024]{1,0:T(8,128)(2,1)S(1)}, u32[]{:S(2)}, u32[]{:S(2)}) collective-permute-start(bf16[256,1024]{1,0:T(8,128)(2,1)S(1)} %collective-permute-done.9.refs_0_), channel_id=1, source_target_pairs={{0,16},{1,9},{2,18},{3,11},{4,20},{5,13},{6,22},{7,15},{8,24},{9,1... | collective-permute-start | bytes 1572872 | tf_op jit(solution)/shard_map/ppermute | solution.py:313
  20.2 5.7 %collective-permute-start.12 = (bf16[128,1536]{1,0:T(8,128)(2,1)S(1)}, bf16[128,1536]{1,0:T(8,128)(2,1)S(1)}, u32[]{:S(2)}, u32[]{:S(2)}) collective-permute-start(bf16[128,1536]{1,0:T(8,128)(2,1)S(1)} %collective-permute-done.refs_3_), channel_id=1, source_target_pairs={{0,1},{1,0},{2,3},{3,2},{4,5},{5,4},{6,7},{7,6},{8,9},{9,8},{10,11... | collective-permute-start | bytes 1179656 | tf_op jit(solution)/shard_map/ppermute | solution.py:296
  20.2 11.1 %collective-permute-start.2 = (bf16[128,1536]{1,0:T(8,128)(2,1)S(1)}, bf16[128,1536]{1,0:T(8,128)(2,1)S(1)}, u32[]{:S(2)}, u32[]{:S(2)}) collective-permute-start(bf16[128,1536]{1,0:T(8,128)(2,1)S(1)} %collective-permute-done.1.refs_7_), channel_id=1, source_target_pairs={{3,1},{4,6},{11,9},{12,14},{19,17},{20,22},{27,25},{28,30}} | collective-permute-start | bytes 1179656 | tf_op jit(solution)/shard_map/ppermute | solution.py:306
  20.9 10.8 %collective-permute-start.6 = (bf16[128,1536]{1,0:T(8,128)(2,1)S(1)}, bf16[128,1536]{1,0:T(8,128)(2,1)S(1)}, u32[]{:S(2)}, u32[]{:S(2)}) collective-permute-start(bf16[128,1536]{1,0:T(8,128)(2,1)S(1)} %collective-permute-done.5.refs_8_), channel_id=1, source_target_pairs={{3,1},{4,6},{11,9},{12,14},{19,17},{20,22},{27,25},{28,30}} | collective-permute-start | bytes 1179656 | tf_op jit(solution)/shard_map/ppermute | solution.py:306
  25.5 10.1 %collective-permute-start.14 = (bf16[128,1536]{1,0:T(8,128)(2,1)S(1)}, bf16[128,1536]{1,0:T(8,128)(2,1)S(1)}, u32[]{:S(2)}, u32[]{:S(2)}) collective-permute-start(bf16[128,1536]{1,0:T(8,128)(2,1)S(1)} %collective-permute-done.1.refs_7_), channel_id=1, source_target_pairs={{0,1},{1,0},{2,3},{3,2},{4,5},{5,4},{6,7},{7,6},{8,9},{9,8},{10,11... | collective-permute-start | bytes 1179656 | tf_op jit(solution)/shard_map/ppermute | solution.py:296
  25.9 9.7 %collective-permute-start.13 = (bf16[128,1536]{1,0:T(8,128)(2,1)S(1)}, bf16[128,1536]{1,0:T(8,128)(2,1)S(1)}, u32[]{:S(2)}, u32[]{:S(2)}) collective-permute-start(bf16[128,1536]{1,0:T(8,128)(2,1)S(1)} %collective-permute-done.4.refs_4_), channel_id=1, source_target_pairs={{0,1},{1,0},{2,3},{3,2},{4,5},{5,4},{6,7},{7,6},{8,9},{9,8},{10,11... | collective-permute-start | bytes 1179656 | tf_op jit(solution)/shard_map/ppermute | solution.py:296
  31.1 4.5 %collective-permute-start.15 = (bf16[128,1536]{1,0:T(8,128)(2,1)S(1)}, bf16[128,1536]{1,0:T(8,128)(2,1)S(1)}, u32[]{:S(2)}, u32[]{:S(2)}) collective-permute-start(bf16[128,1536]{1,0:T(8,128)(2,1)S(1)} %collective-permute-done.5.refs_8_), channel_id=1, source_target_pairs={{0,1},{1,0},{2,3},{3,2},{4,5},{5,4},{6,7},{7,6},{8,9},{9,8},{10,11... | collective-permute-start | bytes 1179656 | tf_op jit(solution)/shard_map/ppermute | solution.py:296
  31.2 5.5 %collective-permute-start.7 = (bf16[128,1536]{1,0:T(8,128)(2,1)S(1)}, bf16[128,1536]{1,0:T(8,128)(2,1)S(1)}, u32[]{:S(2)}, u32[]{:S(2)}) collective-permute-start(bf16[128,1536]{1,0:T(8,128)(2,1)S(1)} %collective-permute-done.2.refs_0_), channel_id=1, source_target_pairs={{0,1},{1,0},{2,3},{3,2},{4,5},{5,4},{6,7},{7,6},{8,9},{9,8},{10,11... | collective-permute-start | bytes 1179656 | tf_op jit(solution)/shard_map/ppermute | solution.py:296
  31.6 5.1 %collective-permute-start.8 = (bf16[128,1536]{1,0:T(8,128)(2,1)S(1)}, bf16[128,1536]{1,0:T(8,128)(2,1)S(1)}, u32[]{:S(2)}, u32[]{:S(2)}) collective-permute-start(bf16[128,1536]{1,0:T(8,128)(2,1)S(1)} %collective-permute-done.6.refs_1_), channel_id=1, source_target_pairs={{0,1},{1,0},{2,3},{3,2},{4,5},{5,4},{6,7},{7,6},{8,9},{9,8},{10,11... | collective-permute-start | bytes 1179656 | tf_op jit(solution)/shard_map/ppermute | solution.py:296
  42.9 4.8 %collective-permute-start.16 = (f32[4,12,128]{2,1,0:T(8,128)S(1)}, f32[4,12,128]{2,1,0:T(8,128)S(1)}, u32[]{:S(2)}, u32[]{:S(2)}) collective-permute-start(f32[4,12,128]{2,1,0:T(8,128)S(1)} %get-tuple-element.20.mine), channel_id=1, source_target_pairs={{0,2},{1,3},{2,0},{3,1},{4,6},{5,7},{6,4},{7,5},{8,10},{9,11},{10,... | collective-permute-start | bytes 73736 | tf_op jit(solution)/shard_map/ppermute | solution.py:324
  47.7 5.0 %collective-permute-start.17 = (f32[4,12,128]{2,1,0:T(8,128)S(1)}, f32[4,12,128]{2,1,0:T(8,128)S(1)}, u32[]{:S(2)}, u32[]{:S(2)}) collective-permute-start(f32[4,12,128]{2,1,0:T(8,128)S(1)} %merge.8.mine), channel_id=1, source_target_pairs={{0,4},{1,5},{2,6},{3,7},{4,0},{5,1},{6,2},{7,3},{8,12},{9,13},{10,... | collective-permute-start | bytes 73736 | tf_op jit(solution)/shard_map/ppermute | solution.py:324
  50.6 3.7 %collective-permute-start.19 = (f32[4,8,128]{2,1,0:T(8,128)S(1)}, f32[4,8,128]{2,1,0:T(8,128)S(1)}, u32[]{:S(2)}, u32[]{:S(2)}) collective-permute-start(f32[4,8,128]{2,1,0:T(8,128)S(1)} %get-tuple-element.21.mine), channel_id=1, source_target_pairs={{0,8},{8,0},{16,24},{24,16},{1,9},{9,1},{17,25},{25,17},{2,10},{10... | collective-permute-start | bytes 49160 | tf_op jit(solution)/shard_map/ppermute | solution.py:327
  52.7 5.4 %collective-permute-start.18 = (f32[4,12,128]{2,1,0:T(8,128)S(1)}, f32[4,12,128]{2,1,0:T(8,128)S(1)}, u32[]{:S(2)}, u32[]{:S(2)}) collective-permute-start(f32[4,12,128]{2,1,0:T(8,128)S(1)} %merge.9.fwd_mine), channel_id=1, source_target_pairs={{0,1},{1,0},{2,3},{3,2},{4,5},{5,4},{6,7},{7,6},{8,9},{9,8},{10,11... | collective-permute-start | bytes 73736 | tf_op jit(solution)/shard_map/ppermute | solution.py:296
  54.4 3.7 %collective-permute-start.20 = (f32[4,8,128]{2,1,0:T(8,128)S(1)}, f32[4,8,128]{2,1,0:T(8,128)S(1)}, u32[]{:S(2)}, u32[]{:S(2)}) collective-permute-start(f32[4,8,128]{2,1,0:T(8,128)S(1)} %merge.10.mine), channel_id=1, source_target_pairs={{0,16},{8,24},{16,0},{24,8},{1,17},{9,25},{17,1},{25,9},{2,18},{10... | collective-permute-start | bytes 49160 | tf_op jit(solution)/shard_map/ppermute | solution.py:327
  61.9 4.0 %collective-permute-start.21 = (f32[4,12,128]{2,1,0:T(8,128)S(1)}, f32[4,12,128]{2,1,0:T(8,128)S(1)}, u32[]{:S(2)}, u32[]{:S(2)}) collective-permute-start(f32[4,12,128]{2,1,0:T(8,128)S(1)} %get-tuple-element.22.mine), channel_id=1, source_target_pairs={{0,2},{1,3},{2,0},{3,1},{4,6},{5,7},{6,4},{7,5},{8,10},{9,11},{10,... | collective-permute-start | bytes 73736 | tf_op jit(solution)/shard_map/ppermute | solution.py:324
  65.9 4.9 %collective-permute-start.22 = (f32[4,12,128]{2,1,0:T(8,128)S(1)}, f32[4,12,128]{2,1,0:T(8,128)S(1)}, u32[]{:S(2)}, u32[]{:S(2)}) collective-permute-start(f32[4,12,128]{2,1,0:T(8,128)S(1)} %merge.12.mine), channel_id=1, source_target_pairs={{0,4},{1,5},{2,6},{3,7},{4,0},{5,1},{6,2},{7,3},{8,12},{9,13},{10,... | collective-permute-start | bytes 73736 | tf_op jit(solution)/shard_map/ppermute | solution.py:324
  67.2 3.7 %collective-permute-start.24 = (f32[4,8,128]{2,1,0:T(8,128)S(1)}, f32[4,8,128]{2,1,0:T(8,128)S(1)}, u32[]{:S(2)}, u32[]{:S(2)}) collective-permute-start(f32[4,8,128]{2,1,0:T(8,128)S(1)} %get-tuple-element.23.mine), channel_id=1, source_target_pairs={{0,8},{8,0},{16,24},{24,16},{1,9},{9,1},{17,25},{25,17},{2,10},{10... | collective-permute-start | bytes 49160 | tf_op jit(solution)/shard_map/ppermute | solution.py:327
  70.8 3.9 %collective-permute-start.23 = (f32[4,12,128]{2,1,0:T(8,128)S(1)}, f32[4,12,128]{2,1,0:T(8,128)S(1)}, u32[]{:S(2)}, u32[]{:S(2)}) collective-permute-start(f32[4,12,128]{2,1,0:T(8,128)S(1)} %merge.13.fwd_mine), channel_id=1, source_target_pairs={{0,1},{1,0},{2,3},{3,2},{4,5},{5,4},{6,7},{7,6},{8,9},{9,8},{10,11... | collective-permute-start | bytes 73736 | tf_op jit(solution)/shard_map/ppermute | solution.py:296
  71.0 3.7 %collective-permute-start.25 = (f32[4,8,128]{2,1,0:T(8,128)S(1)}, f32[4,8,128]{2,1,0:T(8,128)S(1)}, u32[]{:S(2)}, u32[]{:S(2)}) collective-permute-start(f32[4,8,128]{2,1,0:T(8,128)S(1)} %merge.14.mine), channel_id=1, source_target_pairs={{0,16},{8,24},{16,0},{24,8},{1,17},{9,25},{17,1},{25,9},{2,18},{10... | collective-permute-start | bytes 49160 | tf_op jit(solution)/shard_map/ppermute | solution.py:327
